TPU v7x, 32 devices: a whole 2x2x4 slice. The times are simulated.
32 devices in a mesh: row: 4 (over y, core), col: 4 (over z), dev: 2 (over x).
Axes of the slice: x: 2, y: 2, z: 4, core: 2. Of those that a mesh axis runs over, the one named last changes fastest.
Arguments:
- iterate: bfloat16 [64, 4, 4, 1024], P('dev', 'row', 'col'), may hold values from -6 to 6
- right_side: bfloat16 [64, 4, 4, 1024], P('dev', 'row', 'col'), may hold values from -6 to 6
- kernel: bfloat16 [2559], replicated, may hold values from -0.15625 to 0.15625
- inverse_rows: bfloat16 [4, 4, 1024, 1536], P('row', 'col'), may hold values from -0.1875 to 0.1875
- coarse_inverse: bfloat16 [512, 512], P('col', ('row', 'dev')), may hold values from -0.046875 to 0.046875
- aggregate: int32 [4, 4, 1024], P('row', 'col'), may hold values from 0 to 31
- send_index: int32 [4, 4, 4, 128], P('row', 'col'), may hold values from 0 to 1023
Outputs:
- correction: bfloat16 [64, 4, 4, 1024], P('dev', 'row', 'col')
Inputs may be any that keep to these rules, and one draw needn't show every extreme that they name: `send_index`: repeats may occur within one list.
All inputs are finite; a program needn't handle non-finite values.
Results may differ from a plain program's by a relative error of at most 0.0057.
Values may be sent and summed in bfloat16 or wider, within the bound.
No kernel may reach another device: no remote copies, remote signals or barrier semaphores. Data moves between devices by JAX's collectives and lax.ppermute only.
A program may use at most 64 MiB of HBM per device.

v0:
```python
import jax
import jax.numpy as jnp
from jax import lax
from jax.sharding import PartitionSpec as P

NK = 32


def with_halo(block, sides, width):
    for axis, dim in sides:
        count = lax.axis_size(axis)
        forward = [(i, i + 1) for i in range(count - 1)]
        forward.append((count - 1, 0))
        backward = [(target, source) for source, target in forward]
        low = lax.ppermute(
            lax.slice_in_dim(block, block.shape[dim] - width, None, axis=dim), axis, forward
        )
        high = lax.ppermute(lax.slice_in_dim(block, 0, width, axis=dim), axis, backward)
        block = jnp.concatenate([low, block, high], axis=dim)
    return block


def banded(kernel, n_core, n_patch):
    length = kernel.shape[0]
    rolled = jnp.roll(kernel, -(n_core - 1))
    flat = jnp.tile(rolled, n_core)[: n_core * (length - 1)]
    return flat.reshape(n_core, length - 1)[:, :n_patch]


def per_device(iterate, right_side, kernel, inverse_rows, coarse_inverse, aggregate, send_index):
    own_cells = iterate[:, 0, 0, :]
    right_local = right_side[:, 0, 0, :]
    inverse = inverse_rows[0, 0]
    labels = aggregate[0, 0]
    send_rows = send_index[0, 0]
    n_rhs, n_core = own_cells.shape
    n_shell = send_rows.shape[1]
    n_patch = inverse.shape[1]
    outgoing = jnp.transpose(own_cells[:, send_rows], (1, 0, 2))
    padded = with_halo(outgoing[None, None], (("row", 0), ("col", 1)), 1)
    shells = [padded[0, 1, 0], padded[2, 1, 1], padded[1, 0, 2], padded[1, 2, 3]]
    patch_cells = jnp.concatenate([own_cells] + shells, axis=1)
    band = banded(kernel, n_core, n_patch)
    field = lax.dot_general(
        patch_cells, band, (((1,), (1,)), ((), ())), preferred_element_type=jnp.float32
    )
    residual = (right_local.astype(jnp.float32) - own_cells.astype(jnp.float32) - field).astype(
        jnp.bfloat16
    )
    local = jnp.dot(residual, inverse, preferred_element_type=jnp.float32).astype(jnp.bfloat16)
    member = labels[None, :] == lax.broadcasted_iota(jnp.int32, (NK, n_core), 0)
    coarse = lax.dot_general(
        member.astype(jnp.bfloat16),
        residual,
        (((1,), (1,)), ((), ())),
        preferred_element_type=jnp.float32,
    ).astype(jnp.bfloat16)
    n_bx = coarse_inverse.shape[0] // NK
    gathered = lax.all_gather(coarse, "row", axis=1, tiled=True)
    stacked_rhs = gathered.reshape(NK, n_bx, n_rhs)
    paired = lax.all_gather(coarse_inverse, "dev", axis=1, tiled=True)
    n_pair = lax.axis_size("dev")
    n_by = paired.shape[1] // NK
    tiles = paired.reshape(n_bx, NK, n_pair, n_by, NK // n_pair)
    partial_value = jnp.einsum(
        "kxr,xkdym->ydmr", stacked_rhs, tiles, preferred_element_type=jnp.float32
    ).reshape(n_by * NK, n_rhs)
    solved = lax.psum_scatter(partial_value, "col", scatter_dimension=0, tiled=True)
    coarse_part = lax.dot_general(
        solved,
        member.astype(jnp.float32),
        (((0,), (0,)), ((), ())),
        precision=lax.Precision.HIGHEST,
    )
    back_cells = jnp.transpose(local[:, n_core:].reshape(n_rhs, 4, n_shell), (1, 0, 2))
    padded_back = with_halo(back_cells[None, None], (("row", 0), ("col", 1)), 1)
    arrivals = jnp.stack(
        [padded_back[2, 1, 0], padded_back[0, 1, 1], padded_back[1, 2, 2], padded_back[1, 0, 3]]
    )
    placing = (
        send_rows[:, :, None] == lax.broadcasted_iota(jnp.int32, (4, n_shell, n_core), 2)
    ).astype(jnp.bfloat16)
    added = lax.dot_general(
        arrivals, placing, (((0, 2), (0, 1)), ((), ())), preferred_element_type=jnp.float32
    )
    total = local[:, :n_core].astype(jnp.float32) + added + coarse_part
    return total.astype(jnp.bfloat16)[:, None, None, :]


def solution(mesh):
    in_specs = (
        P("dev", "row", "col", None),
        P("dev", "row", "col", None),
        P(),
        P("row", "col", None, None),
        P("col", ("row", "dev")),
        P("row", "col", None),
        P("row", "col", None, None),
    )
    out_specs = P("dev", "row", "col", None)
    return jax.shard_map(
        per_device, mesh=mesh, in_specs=in_specs, out_specs=out_specs, check_vma=False
    )
```

profile of v0, /device:TPU:0, one launch (start us, length us, event | category | flops | bytes accessed | tf_op | source)
XLA Modules:
  0.0 100.4 jit_solution(6350022022780359339)
XLA Ops:
  6.5 1.2 %copy.25 = bf16[32,1024]{0,1:T(8,128)(2,1)S(1)} copy(bf16[32,1024]{1,0:T(8,128)(2,1)} %bitcast.77) | data formatting | bytes 131072 | tf_op jit(solution)/shard_map/squeeze | solution.py:31
  7.7 0.7 fusion.29
  8.4 1.3 %gather_fusion = bf16[512,32]{1,0:T(8,128)(2,1)S(1)} fusion(bf16[32,1024]{0,1:T(8,128)(2,1)S(1)} %copy.25, s32[1024]{0:T(1024)S(1)} %pad_clamp_fusion), kind=kCustom, calls=%fused_computation | custom fusion | bytes 67584 | tf_op jit(solution)/shard_map/gather | solution.py:39
  9.8 0.5 collective-permute-start
  10.4 2.0 %collective-permute-start.1 = (bf16[1,1,4,32,128]{4,3,2,1,0:T(8,128)(2,1)S(1)}, bf16[1,1,4,32,128]{4,3,2,1,0:T(8,128)(2,1)S(1)}, u32[]{:S(2)}, u32[]{:S(2)}) collective-permute-start(bf16[1,1,4,32,128]{4,3,2,1,0:T(8,128)(2,1)S(1)} %bitcast.82), channel_id=1, source_target_pairs={{8,0},{16,8},{24,16},{0,24},{9,1},{17,9},{25,17},{1,25},{10,2},{18... | collective-permute-start | bytes 98312 | tf_op jit(solution)/shard_map/ppermute | solution.py:18
  12.4 1.5 %constant_dynamic-update-slice_fusion.4 = bf16[32,1536]{1,0:T(8,128)(2,1)} fusion(bf16[32,1,1,1024]{3,0,2,1:T(8,128)(2,1)} %param.7), kind=kLoop, calls=%fused_computation.38 | loop fusion | bytes 131072
  13.9 0.8 slice.48
  14.6 0.7 slice.49
  15.3 2.7 %tile.4 = bf16[1024,2559]{1,0:T(8,128)(2,1)} broadcast(bf16[2559]{0:T(1024)(128)(2,1)S(1)} %pad_maximum_fusion.2), dimensions={1} | broadcast | bytes 5245950 | tf_op jit(solution)/shard_map/tile | solution.py:26
  18.0 13.1 %tile.10 = bf16[2620416]{0:T(1024)(128)(2,1)} reshape(bf16[1024,2559]{1,0:T(8,128)(2,1)} %tile.4) | data formatting | bytes 10481664 | tf_op jit(solution)/shard_map/tile | solution.py:26
  31.1 5.8 %slice.64 = bf16[2619392]{0:T(1024)(128)(2,1)} slice(bf16[2620416]{0:T(1024)(128)(2,1)} %tile.10), slice={[0:2619392]} | slice | bytes 10477568 | tf_op jit(solution)/shard_map/slice | solution.py:26
  36.9 11.3 %reshape.48 = bf16[1024,2558]{1,0:T(8,128)(2,1)} reshape(bf16[2619392]{0:T(1024)(128)(2,1)} %slice.64) | data formatting | bytes 10477568 | tf_op jit(solution)/shard_map/reshape | solution.py:27
  48.2 4.6 %all_gather.7 = bf16[128,128]{0,1:T(8,128)(2,1)S(1)} all-gather(bf16[128,64]{0,1:T(8,128)(2,1)S(1)} %copy-done.2), channel_id=1, replica_groups=mesh['row'=4,'col'=4,'dev'=2] {'dev'}, dimensions={1}, use_global_device_ids=true | all-gather | bytes 49152 | tf_op jit(solution)/shard_map/all_gather | solution.py:61
  52.9 2.2 %collective-permute-start.2 = (bf16[3,1,4,32,128]{4,3,2,1,0:T(8,128)(2,1)S(1)}, bf16[3,1,4,32,128]{4,3,2,1,0:T(8,128)(2,1)S(1)}, u32[]{:S(2)}, u32[]{:S(2)}) collective-permute-start(bf16[3,1,4,32,128]{4,3,2,1,0:T(8,128)(2,1)S(1)} %pad_maximum_fusion), channel_id=1, source_target_pairs={{0,2},{2,4},{4,6},{6,0},{1,3},{3,5},{5,7},{7,1},{8,10},{10,12},{12... | collective-permute-start | bytes 294920 | tf_op jit(solution)/shard_map/ppermute | solution.py:15
  55.1 2.1 %collective-permute-start.3 = (bf16[3,1,4,32,128]{4,3,2,1,0:T(8,128)(2,1)S(1)}, bf16[3,1,4,32,128]{4,3,2,1,0:T(8,128)(2,1)S(1)}, u32[]{:S(2)}, u32[]{:S(2)}) collective-permute-start(bf16[3,1,4,32,128]{4,3,2,1,0:T(8,128)(2,1)S(1)} %pad_maximum_fusion), channel_id=1, source_target_pairs={{2,0},{4,2},{6,4},{0,6},{3,1},{5,3},{7,5},{1,7},{10,8},{12,10},{14... | collective-permute-start | bytes 294920 | tf_op jit(solution)/shard_map/ppermute | solution.py:18
  57.2 0.6 constant_dynamic-update-slice_fusion.3
  57.8 0.6 constant_dynamic-update-slice_fusion.2
  58.4 2.0 %collective-permute-done.2 = bf16[3,1,4,32,128]{4,3,2,1,0:T(8,128)(2,1)S(1)} collective-permute-done((bf16[3,1,4,32,128]{4,3,2,1,0:T(8,128)(2,1)S(1)}, bf16[3,1,4,32,128]{4,3,2,1,0:T(8,128)(2,1)S(1)}, u32[]{:S(2)}, u32[]{:S(2)}) %collective-permute-start.2) | collective-permute-done | bytes 98336 | tf_op jit(solution)/shard_map/ppermute | solution.py:15
  60.4 0.6 constant_dynamic-update-slice_fusion.1
  61.0 0.6 constant_dynamic-update-slice_fusion
  61.6 2.9 %fusion.13 = bf16[32,1024]{1,0:T(8,128)(2,1)S(1)} fusion(bf16[32,1536]{1,0:T(8,128)(2,1)} %constant_dynamic-update-slice_fusion, bf16[1024,2558]{1,0:T(8,128)(2,1)} %reshape.48, bf16[32,1,1,1024]{3,0,2,1:T(8,128)(2,1)} %param.8, bf16[32,1,1,1024]{3,0,2,1:T(8,128)(2,1)S(1)} %copy-done.1), kind=kOutput, calls=%fused_computation.12 | convolution fusion | flops 100827136 | bytes 3440640 | tf_op jit(solution)/shard_map/dot_general | solution.py:44
  64.6 0.6 fusion.4
  65.3 0.5 collective-permute-start.5
  66.0 5.3 %all_gather.6 = bf16[32,128]{0,1:T(8,128)(2,1)S(1)} all-gather(bf16[32,32]{0,1:T(8,128)(2,1)S(1)} %copy.29), channel_id=1, replica_groups=mesh['row'=4,'col'=4,'dev'=2] {'row'}, dimensions={1}, use_global_device_ids=true | all-gather | bytes 10240 | tf_op jit(solution)/shard_map/all_gather | solution.py:59
  71.3 0.2 convolution_bitcast_fusion
  71.5 0.6 copy.33
  72.2 0.8 collective-permute-start.7
  73.0 3.0 %collective-permute-start.6 = (bf16[3,1,4,32,128]{4,3,2,1,0:T(8,128)(2,1)S(1)}, bf16[3,1,4,32,128]{4,3,2,1,0:T(8,128)(2,1)S(1)}, u32[]{:S(2)}, u32[]{:S(2)}) collective-permute-start(bf16[3,1,4,32,128]{4,3,2,1,0:T(8,128)(2,1)S(1)} %pad_maximum_fusion.1), channel_id=1, source_target_pairs={{2,0},{4,2},{6,4},{0,6},{3,1},{5,3},{7,5},{1,7},{10,8},{12,10},{14... | collective-permute-start | bytes 294920 | tf_op jit(solution)/shard_map/ppermute | solution.py:18
  76.0 3.7 %collective-permute-done.7 = bf16[3,1,4,32,128]{4,3,2,1,0:T(8,128)(2,1)S(1)} collective-permute-done((bf16[3,1,4,32,128]{4,3,2,1,0:T(8,128)(2,1)S(1)}, bf16[3,1,4,32,128]{4,3,2,1,0:T(8,128)(2,1)S(1)}, u32[]{:S(2)}, u32[]{:S(2)}) %collective-permute-start.7) | collective-permute-done | bytes 98336 | tf_op jit(solution)/shard_map/ppermute | solution.py:15
  79.9 0.5 fusion.12
  80.4 11.5 %reduce-scatter.2.cloned.1.call-done = f32[32,32]{1,0:T(8,128)} async-done(((f32[128,32]{1,0:T(8,128)}), f32[32,32]{1,0:T(8,128)}) %reduce-scatter.2.cloned.1.call-update) | async-done | bytes 4112 | tf_op jit(solution)/shard_map/reduce_scatter | solution.py:68
  91.9 1.6 %fusion.17 = bf16[32,1,1,1024]{3,0,2,1:T(8,128)(2,1)} fusion(f32[32,1024]{1,0:T(8,128)S(1)} %fusion.12, f32[32,32]{1,0:T(8,128)} %reduce-scatter.2.cloned.1.call-done, s32[1024]{0:T(1024)S(1)} %bitcast.85), kind=kOutput, calls=%fused_computation.14 | convolution fusion | flops 12681216 | bytes 204800 | tf_op jit(solution)/shard_map/dot_general | solution.py:69
  (32 shorter events, 0.7 us)
Async XLA Ops:
  6.5 58.0 %copy-start = (bf16[1,1,1024,1536]{3,2,1,0:T(8,128)(2,1)S(1)}, bf16[1,1,1024,1536]{3,2,1,0:T(8,128)(2,1)}, u32[]{:S(2)}) copy-start(bf16[1,1,1024,1536]{3,2,1,0:T(8,128)(2,1)} %param.10) | copy-start | bytes 9437188
  6.5 85.4 %reduce-scatter.2.cloned.1.call-start = ((), (), s32[]{:S(2)}) async-start(), calls=%async_computation.1 | async-start | bytes 81920 | tf_op jit(solution)/shard_map/reduce_scatter | solution.py:68
  9.8 43.1 %collective-permute-start = (bf16[1,1,4,32,128]{4,3,2,1,0:T(8,128)(2,1)S(1)}, bf16[1,1,4,32,128]{4,3,2,1,0:T(8,128)(2,1)S(1)}, u32[]{:S(2)}, u32[]{:S(2)}) collective-permute-start(bf16[1,1,4,32,128]{4,3,2,1,0:T(8,128)(2,1)S(1)} %bitcast.81), channel_id=1, source_target_pairs={{0,8},{8,16},{16,24},{24,0},{1,9},{9,17},{17,25},{25,1},{2,10},{10... | collective-permute-start | bytes 98312 | tf_op jit(solution)/shard_map/ppermute | solution.py:15
  10.4 42.5 %collective-permute-start.1 = (bf16[1,1,4,32,128]{4,3,2,1,0:T(8,128)(2,1)S(1)}, bf16[1,1,4,32,128]{4,3,2,1,0:T(8,128)(2,1)S(1)}, u32[]{:S(2)}, u32[]{:S(2)}) collective-permute-start(bf16[1,1,4,32,128]{4,3,2,1,0:T(8,128)(2,1)S(1)} %bitcast.82), channel_id=1, source_target_pairs={{8,0},{16,8},{24,16},{0,24},{9,1},{17,9},{25,17},{1,25},{10,2},{18... | collective-permute-start | bytes 98312 | tf_op jit(solution)/shard_map/ppermute | solution.py:18
  36.9 11.3 %copy-start.2 = (bf16[128,64]{0,1:T(8,128)(2,1)S(1)}, bf16[128,64]{0,1:T(8,128)(2,1)}, u32[]{:S(2)}) copy-start(bf16[128,64]{0,1:T(8,128)(2,1)} %param.11) | copy-start | bytes 49156
  36.9 24.8 %copy-start.1 = (bf16[32,1,1,1024]{3,0,2,1:T(8,128)(2,1)S(1)}, bf16[32,1,1,1024]{3,0,2,1:T(8,128)(2,1)}, u32[]{:S(2)}) copy-start(bf16[32,1,1,1024]{3,0,2,1:T(8,128)(2,1)} %param.7) | copy-start | bytes 196612
  52.9 7.5 %collective-permute-start.2 = (bf16[3,1,4,32,128]{4,3,2,1,0:T(8,128)(2,1)S(1)}, bf16[3,1,4,32,128]{4,3,2,1,0:T(8,128)(2,1)S(1)}, u32[]{:S(2)}, u32[]{:S(2)}) collective-permute-start(bf16[3,1,4,32,128]{4,3,2,1,0:T(8,128)(2,1)S(1)} %pad_maximum_fusion), channel_id=1, source_target_pairs={{0,2},{2,4},{4,6},{6,0},{1,3},{3,5},{5,7},{7,1},{8,10},{10,12},{12... | collective-permute-start | bytes 294920 | tf_op jit(solution)/shard_map/ppermute | solution.py:15
  55.1 5.9 %collective-permute-start.3 = (bf16[3,1,4,32,128]{4,3,2,1,0:T(8,128)(2,1)S(1)}, bf16[3,1,4,32,128]{4,3,2,1,0:T(8,128)(2,1)S(1)}, u32[]{:S(2)}, u32[]{:S(2)}) collective-permute-start(bf16[3,1,4,32,128]{4,3,2,1,0:T(8,128)(2,1)S(1)} %pad_maximum_fusion), channel_id=1, source_target_pairs={{2,0},{4,2},{6,4},{0,6},{3,1},{5,3},{7,5},{1,7},{10,8},{12,10},{14... | collective-permute-start | bytes 294920 | tf_op jit(solution)/shard_map/ppermute | solution.py:18
  61.6 4.2 %copy-start.3 = (s32[1,1,1024]{2,1,0:T(1,128)S(1)}, s32[1,1,1024]{2,1,0:T(1,128)}, u32[]{:S(2)}) copy-start(s32[1,1,1024]{2,1,0:T(1,128)} %param.12) | copy-start | bytes 12292
  61.6 18.3 %copy-start.4 = (s32[1,1,4,128]{3,2,1,0:T(4,128)S(1)}, s32[1,1,4,128]{3,2,1,0:T(4,128)}, u32[]{:S(2)}) copy-start(s32[1,1,4,128]{3,2,1,0:T(4,128)} %param.13) | copy-start | bytes 6148
  65.2 6.9 %collective-permute-start.4 = (bf16[1,1,4,32,128]{4,3,2,1,0:T(8,128)(2,1)S(1)}, bf16[1,1,4,32,128]{4,3,2,1,0:T(8,128)(2,1)S(1)}, u32[]{:S(2)}, u32[]{:S(2)}) collective-permute-start(bf16[1,1,4,32,128]{4,3,2,1,0:T(8,128)(2,1)S(1)} %bitcast_bitcast_fusion), channel_id=1, source_target_pairs={{8,0},{16,8},{24,16},{0,24},{9,1},{17,9},{25,17},{1,25},{10,2},{18... | collective-permute-start | bytes 98312 | tf_op jit(solution)/shard_map/ppermute | solution.py:18
  65.3 6.8 %collective-permute-start.5 = (bf16[1,1,4,32,128]{4,3,2,1,0:T(8,128)(2,1)S(1)}, bf16[1,1,4,32,128]{4,3,2,1,0:T(8,128)(2,1)S(1)}, u32[]{:S(2)}, u32[]{:S(2)}) collective-permute-start(bf16[1,1,4,32,128]{4,3,2,1,0:T(8,128)(2,1)S(1)} %bitcast_bitcast_fusion), channel_id=1, source_target_pairs={{0,8},{8,16},{16,24},{24,0},{1,9},{9,17},{17,25},{25,1},{2,10},{10... | collective-permute-start | bytes 98312 | tf_op jit(solution)/shard_map/ppermute | solution.py:15
  72.2 7.6 %collective-permute-start.7 = (bf16[3,1,4,32,128]{4,3,2,1,0:T(8,128)(2,1)S(1)}, bf16[3,1,4,32,128]{4,3,2,1,0:T(8,128)(2,1)S(1)}, u32[]{:S(2)}, u32[]{:S(2)}) collective-permute-start(bf16[3,1,4,32,128]{4,3,2,1,0:T(8,128)(2,1)S(1)} %pad_maximum_fusion.1), channel_id=1, source_target_pairs={{0,2},{2,4},{4,6},{6,0},{1,3},{3,5},{5,7},{7,1},{8,10},{10,12},{12... | collective-permute-start | bytes 294920 | tf_op jit(solution)/shard_map/ppermute | solution.py:15
  73.0 6.9 %collective-permute-start.6 = (bf16[3,1,4,32,128]{4,3,2,1,0:T(8,128)(2,1)S(1)}, bf16[3,1,4,32,128]{4,3,2,1,0:T(8,128)(2,1)S(1)}, u32[]{:S(2)}, u32[]{:S(2)}) collective-permute-start(bf16[3,1,4,32,128]{4,3,2,1,0:T(8,128)(2,1)S(1)} %pad_maximum_fusion.1), channel_id=1, source_target_pairs={{2,0},{4,2},{6,4},{0,6},{3,1},{5,3},{7,5},{1,7},{10,8},{12,10},{14... | collective-permute-start | bytes 294920 | tf_op jit(solution)/shard_map/ppermute | solution.py:18
Sparse Core Ops, SparseCore 0:
  72.2 19.6 reduce-scatter.1
where the time goes:
time: 101 us; the launch traced here: 100 us
  local copies, waits for them, and re-layouts  41.7 us (41%)
  waiting for transfers between devices  17.3 us (17%)
  between operations  13.5 us (13%)
  starting transfers between devices  11.3 us (11%)
  blocking collectives  9.83 us (10%)
  matrix products  6 us (6%)
    another operation x2, local copies, waits for them, and re-layouts, banded(): flat = jnp.tile(rolled, n_core)[:n_core * (length - 1)]  15.8 us
    reduce_scatter x1, waiting for transfers between devices, per_device(): lax.psum_scatter(partial_value, 'col', scatter_dimension=0, tiled=True)  11.5 us
    reshape x1, local copies, waits for them, and re-layouts, banded(): return flat.reshape(n_core, length - 1)[:, :n_patch]  11.3 us
    ppermute x4, starting transfers between devices, with_halo(): lax.ppermute(lax.slice_in_dim(block, 0, width, axis=dim), axis, backward)  7.19 us
    slice x1, local copies, waits for them, and re-layouts, banded(): flat = jnp.tile(rolled, n_core)[:n_core * (length - 1)]  5.78 us
    ppermute x4, waiting for transfers between devices, with_halo(): lax.ppermute(lax.slice_in_dim(block, block.shape[dim] - width, None, axis...  5.69 us
    all_gather x1, blocking collectives, per_device(): gathered = lax.all_gather(coarse, 'row', axis=1, tiled=True)  5.26 us
    all_gather x1, blocking collectives, per_device(): paired = lax.all_gather(coarse_inverse, 'dev', axis=1, tiled=True)  4.57 us
  transfers between devices with their start and end apart: 9, of which 4 were waited for; matrix products, arithmetic and copies ran while one was open for 39% of the time, Pallas kernels for 0%

commit v1 on v0

v1 whole, which is shorter than its diff:
```python
import functools

import jax
import jax.numpy as jnp
from jax import lax
from jax.experimental import pallas as pl
from jax.experimental.pallas import tpu as pltpu
from jax.sharding import PartitionSpec as P

LANES = 128
BLOCK = 256
VMEM = pl.BlockSpec(memory_space=pltpu.VMEM)
HBM = pl.BlockSpec(memory_space=pltpu.HBM)
F32 = jnp.float32
BF16 = jnp.bfloat16


def mm(left, right):
    return jnp.dot(left, right, preferred_element_type=F32)


def mm_nt(left, right):
    return lax.dot_general(left, right, (((1,), (1,)), ((), ())), preferred_element_type=F32)


def one_hot(labels, rows):
    shape = (rows, labels.shape[1])
    hit = lax.broadcasted_iota(jnp.int32, shape, 0) == jnp.broadcast_to(labels, shape)
    return jnp.where(hit, 1.0, 0.0).astype(BF16)


def place(axis):
    index = lax.axis_index(axis)
    return index, lax.rem(index, 2), lax.axis_size(axis)


def partners(axis):
    index, odd, count = place(axis)
    outer = lax.rem(index + jnp.where(odd == 1, 1, count - 1), count)
    inner = index + jnp.where(odd == 1, -1, 1)
    return [index, outer, inner] + [lax.rem(index + o, count) for o in range(2, count - 1)]


def outer_pairs(count):
    return [(i, (i + 1) % count if i % 2 else (i - 1) % count) for i in range(count)]


def inner_pairs(count):
    return [(i, i ^ 1) for i in range(count)]


def shifted(count, step):
    return [(i, (i + step) % count) for i in range(count)]


def gather_kernel(own_hbm, send_hbm, right_hbm, labels_hbm, columns_hbm, co, ro, ci, ri, spots_ref, own_ref, right_ref, labels_ref, columns_ref, send_ref, sems):
    pairs = (
        (send_hbm, send_ref),
        (own_hbm, own_ref),
        (right_hbm, right_ref),
        (labels_hbm, labels_ref),
        (columns_hbm, columns_ref),
    )
    copies = [pltpu.make_async_copy(a, b, sems.at[i]) for i, (a, b) in enumerate(pairs)]
    for copy in copies:
        copy.start()
    copies[0].wait()
    n_core = own_ref.shape[1]
    shell = send_ref.shape[1]
    hots = []
    for slot, (axis, base, inner) in enumerate((("row", 0, 0), ("row", 0, 1), ("col", 2, 0), ("col", 2, 1))):
        odd = place(axis)[1]
        direction = base + jnp.where(odd == 1, inner, 1 - inner)
        hot = one_hot(send_ref[pl.ds(direction, 1), :], n_core)
        spots_ref[:, slot * shell : (slot + 1) * shell] = hot
        hots.append(hot)
    copies[1].wait()
    own = own_ref[...]
    for slot, out in ((2, co), (0, ro), (3, ci), (1, ri)):
        out[...] = mm(own, spots_ref[:, slot * shell : (slot + 1) * shell]).astype(BF16)
    for copy in copies[2:]:
        copy.wait()


def strip_kernel(kernel_ref, own_ref, right_ref, inv_hbm, strip_ref, base_ref, inv_ref, sem):
    copy = pltpu.make_async_copy(inv_hbm, inv_ref, sem)
    copy.start()
    width = kernel_ref.shape[1]
    n_core = own_ref.shape[1]
    rows = 16
    row = jnp.broadcast_to(kernel_ref[...], (rows, width))
    first = pltpu.roll(row, 0, 1, stride=1, stride_axis=0)
    for g in range(BLOCK // rows):
        part = first if g == 0 else pltpu.roll(first, g * rows, 1)
        strip_ref[g * rows : (g + 1) * rows, :] = part[:, BLOCK:].astype(BF16)
    own = own_ref[...]
    for b in range(n_core // BLOCK):
        start = n_core - BLOCK - BLOCK * b
        here = slice(b * BLOCK, (b + 1) * BLOCK)
        field = mm_nt(own, strip_ref[:, start : start + n_core])
        base_ref[:, here] = right_ref[:, here].astype(F32) - own[:, here].astype(F32) - field
    copy.wait()


def columns_kernel(labels_ref, *refs):
    n_dev = len(refs) - 2
    parts, columns_ref, member_ref = refs[:n_dev], refs[n_dev], refs[n_dev + 1]
    targets = partners("col")
    half = parts[0].shape[0] // len(targets)
    dev = lax.axis_index("dev")
    columns_ref[...] = jnp.zeros_like(columns_ref)
    for d, by in enumerate(targets):
        source = pl.multiple_of(by * half, half)
        for e in range(n_dev):
            target = pl.multiple_of(lax.rem(dev + e, n_dev) * half, half)
            columns_ref[d, pl.ds(target, half), :] = parts[e][pl.ds(source, half), :]
    member_ref[...] = one_hot(labels_ref[...], member_ref.shape[0])


def residual_kernel(base_ref, to, ti, uo, ui, strip_ref, inv_ref, member_ref, ro, rx, ri, co, ci, res_ref):
    n_core = base_ref.shape[1]
    rows, shell = to.shape
    odd_row, odd_col = place("row")[1] == 1, place("col")[1] == 1
    low = [jnp.where(odd_row, ti[...], to[...]), jnp.where(odd_row, to[...], ti[...])]
    high = [jnp.where(odd_col, ui[...], uo[...]), jnp.where(odd_col, uo[...], ui[...])]
    shells = jnp.concatenate(low + high, axis=1)
    width = shells.shape[1]
    for b in range(n_core // BLOCK):
        start = 2 * n_core - BLOCK - BLOCK * b
        here = slice(b * BLOCK, (b + 1) * BLOCK)
        field = mm_nt(shells, strip_ref[:, start : start + width])
        res_ref[:, here] = (base_ref[:, here] - field).astype(BF16)
    res = res_ref[...]
    coarse = mm_nt(res, member_ref[...]).astype(BF16)
    rx[...] = coarse
    local = mm(res, inv_ref[:, n_core:]).astype(BF16)
    back = [local[:, j * shell : (j + 1) * shell] for j in range(4)]
    ro[:rows, :] = jnp.where(odd_row, back[1], back[0])
    ro[rows:, :] = coarse
    ri[:rows, :] = jnp.where(odd_row, back[0], back[1])
    ri[rows:, :] = coarse
    co[...] = jnp.where(odd_col, back[3], back[2])
    ci[...] = jnp.where(odd_col, back[2], back[3])


def partial_kernel(columns_ref, co, ci, *refs):
    sources = partners("row")
    n_bx = len(sources)
    gathered, outs = refs[:n_bx], refs[n_bx:]
    width = columns_ref.shape[2]
    rows = co.shape[0]
    total = jnp.zeros((rows, width), F32)
    for bx, ref in zip(sources, gathered):
        piece = ref[-rows:, :].astype(F32)
        if width > LANES:
            piece = jnp.concatenate([piece, jnp.zeros((rows, width - LANES), F32)], axis=1)
        total = total + pltpu.roll(piece, bx * (width // n_bx), 1)
    total = total.astype(BF16)
    outs[1][:rows, :] = co[...].astype(F32)
    outs[2][:rows, :] = ci[...].astype(F32)
    for d, out in enumerate(outs):
        out[-rows:, :] = mm_nt(total, columns_ref[d])


def local_kernel(res_ref, inv_ref, spots_ref, ro, ri, acc_ref):
    rows, n_core = res_ref.shape
    arrived = jnp.concatenate([ro[:rows, :], ri[:rows, :]], axis=1)
    added = mm_nt(arrived, spots_ref[:, : arrived.shape[1]])
    acc_ref[...] = mm(res_ref[...], inv_ref[:, :n_core]).astype(BF16).astype(F32) + added


def final_kernel(acc_ref, member_ref, spots_ref, *refs):
    parts, out_ref = refs[:-1], refs[-1]
    rows = acc_ref.shape[0]
    solved = parts[0][...]
    for part in parts[1:]:
        solved = solved + part[-rows:, :]
    high = solved.astype(BF16)
    low = (solved - high.astype(F32)).astype(BF16)
    both = mm(jnp.concatenate([high, low], axis=0), member_ref[...])
    arrived = jnp.concatenate([parts[1][:rows, :], parts[2][:rows, :]], axis=1).astype(BF16)
    added = mm_nt(arrived, spots_ref[:, arrived.shape[1] :])
    out_ref[...] = (acc_ref[...] + added + both[:rows] + both[rows:]).astype(BF16)


def call(body, name, shapes, *args, hbm=(), scratch=(), limit=16, flops=10**6):
    out_shape = [jax.ShapeDtypeStruct(s, t) for s, t in shapes]
    size = sum(a.size * a.dtype.itemsize for a in args)
    return pl.pallas_call(
        body,
        out_shape=out_shape,
        in_specs=[HBM if i in hbm else VMEM for i in range(len(args))],
        out_specs=[VMEM] * len(out_shape),
        scratch_shapes=scratch,
        name=name,
        compiler_params=pltpu.CompilerParams(vmem_limit_bytes=limit << 20),
        cost_estimate=pl.CostEstimate(flops=flops, bytes_accessed=size, transcendentals=0),
    )(*args)


def per_device(iterate, right_side, kernel, inverse_rows, coarse_inverse, aggregate, send_index):
    own = iterate[:, 0, 0, :]
    right = right_side[:, 0, 0, :]
    inverse = inverse_rows[0, 0]
    labels = aggregate[0]
    send = send_index[0, 0]
    mine = coarse_inverse.T
    rows, n_core = own.shape
    n_shell = send.shape[1]
    n_patch = inverse.shape[1]
    n_bx, n_by, n_dev = (lax.axis_size(a) for a in ("row", "col", "dev"))
    coarse_rows = coarse_inverse.shape[0]
    shell = ((rows, n_shell), BF16)
    double = ((2 * rows, LANES), BF16)

    same = [(a.shape, a.dtype) for a in (own, right, labels, mine)]
    co, ro, ci, ri, spots, own, right, labels, mine = call(
        gather_kernel,
        "gather",
        [shell] * 4 + [((n_core, 4 * n_shell), BF16)] + same,
        own,
        send,
        right,
        labels,
        mine,
        hbm=range(5),
        scratch=[pltpu.VMEM(send.shape, send.dtype), pltpu.SemaphoreType.DMA((5,))],
    )
    uo = lax.ppermute(co, "col", outer_pairs(n_by))
    to = lax.ppermute(ro, "row", outer_pairs(n_bx))
    ui = lax.ppermute(ci, "col", inner_pairs(n_by))
    ti = lax.ppermute(ri, "row", inner_pairs(n_bx))
    halves = [mine] + [lax.ppermute(mine, "dev", shifted(n_dev, -e)) for e in range(1, n_dev)]

    width = n_core + n_patch
    padded = jnp.pad(kernel.astype(F32), (1, width - kernel.shape[0] - 1))[None, :]
    strip, base, inverse = call(
        strip_kernel,
        "strip",
        [((BLOCK, width - BLOCK), BF16), ((rows, n_core), F32), (inverse.shape, BF16)],
        padded,
        own,
        right,
        inverse,
        hbm=(3,),
        scratch=[pltpu.SemaphoreType.DMA],
    )
    columns, member = call(
        columns_kernel,
        "columns",
        [((n_by, LANES, coarse_rows), BF16), ((LANES, n_core), BF16)],
        labels,
        *halves,
    )
    ro, rx, ri, co, ci, res = call(
        residual_kernel,
        "residual",
        [double, shell, double, shell, shell, ((rows, n_core), BF16)],
        base,
        to,
        ti,
        uo,
        ui,
        strip,
        inverse,
        member,
    )
    ao = lax.ppermute(ro, "row", outer_pairs(n_bx))
    rest = [lax.ppermute(rx, "row", shifted(n_bx, -o)) for o in range(2, n_bx - 1)]
    ai = lax.ppermute(ri, "row", inner_pairs(n_bx))
    single, wide = ((rows, LANES), F32), ((2 * rows, LANES), F32)
    partials = call(
        partial_kernel,
        "partial",
        [single, wide, wide] + [single] * (n_by - 3),
        columns,
        co,
        ci,
        rx,
        ao,
        ai,
        *rest,
    )
    so = lax.ppermute(partials[1], "col", outer_pairs(n_by))
    others = [lax.ppermute(partials[d + 1], "col", shifted(n_by, d)) for d in range(2, n_by - 1)]
    si = lax.ppermute(partials[2], "col", inner_pairs(n_by))
    (acc,) = call(local_kernel, "local", [((rows, n_core), F32)], res, inverse, spots, ao, ai)
    (out,) = call(final_kernel, "final", [((rows, n_core), BF16)], acc, member, spots, partials[0], so, si, *others)
    return out[:, None, None, :]


def solution(mesh):
    in_specs = (
        P("dev", "row", "col", None),
        P("dev", "row", "col", None),
        P(),
        P("row", "col", None, None),
        P("col", ("row", "dev")),
        P("row", "col", None),
        P("row", "col", None, None),
    )
    out_specs = P("dev", "row", "col", None)
    return jax.shard_map(
        per_device, mesh=mesh, in_specs=in_specs, out_specs=out_specs, check_vma=False
    )
```

time: 101 us -> 30.1 us (0.30)
  local copies, waits for them, and re-layouts: 41.7 us -> 5.66 us
  waiting for transfers between devices: 17.3 us -> 3.83 us
  between operations: 13.5 us -> 0.11 us
  blocking collectives: 9.83 us -> 0 us
  matrix products: 6 us -> 0 us
  Pallas kernels: 0 us -> 4.52 us
  starting transfers between devices: 11.3 us -> 14.8 us
    another operation x6 -> x0, local copies, waits for them, and re-layouts: 15.8 us -> none  [the longest x2 15.8 us: banded(): flat = jnp.tile(rolled, n_core)[:n_core * (length - 1)]]
    reduce_scatter x1 -> x0, waiting for transfers between devices: 11.5 us -> none  [per_device(): lax.psum_scatter(partial_value, 'col', scatter_dimension=0, tiled=True)]
    reshape x2 -> x0, local copies, waits for them, and re-layouts: 11.4 us -> none  [the longest x1 11.3 us: banded(): return flat.reshape(n_core, length - 1)[:, :n_patch]]
    all_gather x2 -> x0, blocking collectives: 9.83 us -> none  [the longest x1 5.26 us: per_device(): gathered = lax.all_gather(coarse, 'row', axis=1, tiled=True)]
    slice x3 -> x0, local copies, waits for them, and re-layouts: 7.23 us -> none  [the longest x1 5.78 us: banded(): flat = jnp.tile(rolled, n_core)[:n_core * (length - 1)]]
    dot_general x6 -> x0, matrix products: 6 us -> none  [the longest x1 2.94 us: per_device(): lax.dot_general(patch_cells, band, (((1,), (1,)), ((), ())), preferred_el...]
    pallas_call x0 -> x7, Pallas kernels: none -> 4.52 us  [call(): pl.pallas_call(body, out_shape=out_shape, in_specs=[HBM if i in hbm else...]
    ppermute x8 -> x11, starting transfers between devices: 11.3 us -> 14.8 us  [the longest x1 3.6 us: per_device(): uo = lax.ppermute(co, 'col', outer_pairs(n_by))]
  transfers between devices with their start and end apart: 9 -> 11, of which waited for: 4 -> 2; matrix products, arithmetic and copies ran while one was open for 39% -> 3% of each run, Pallas kernels for 0% -> 6%
where the time goes in v1:
time: 30.1 us; the launch traced here: 29.7 us
  starting transfers between devices  14.8 us (49%)
  local copies, waits for them, and re-layouts  5.66 us (19%)
  Pallas kernels  4.52 us (15%)
  waiting for transfers between devices  3.83 us (13%)
  other arithmetic  0.76 us (3%)
    unnamed x12, local copies, waits for them, and re-layouts  5.65 us
    pallas_call x7, Pallas kernels, call(): pl.pallas_call(body, out_shape=out_shape, in_specs=[HBM if i in hbm else...  4.52 us
    ppermute x1, starting transfers between devices, per_device(): uo = lax.ppermute(co, 'col', outer_pairs(n_by))  3.6 us
    ppermute x1, starting transfers between devices, per_device(): to = lax.ppermute(ro, 'row', outer_pairs(n_bx))  2.5 us
    ppermute x1, starting transfers between devices, per_device(): lax.ppermute(partials[d + 1], 'col', shifted(n_by, d))  2.34 us
    ppermute x1, waiting for transfers between devices, per_device(): lax.ppermute(rx, 'row', shifted(n_bx, -o))  2.13 us
    ppermute x1, waiting for transfers between devices, per_device(): lax.ppermute(partials[d + 1], 'col', shifted(n_by, d))  1.67 us
    ppermute x1, starting transfers between devices, per_device(): lax.ppermute(rx, 'row', shifted(n_bx, -o))  1.52 us
  transfers between devices with their start and end apart: 11, of which 2 were waited for; matrix products, arithmetic and copies ran while one was open for 3% of the time, Pallas kernels for 6%

profile of v1, /device:TPU:0, one launch (start us, length us, event | category | flops | bytes accessed | tf_op | source)
XLA Modules:
  0.0 29.7 jit_solution(12109933683842408425)
XLA Ops:
  0.0 0.8 %copy-done.1 = bf16[32,1,1,1024]{3,0,2,1:T(8,128)(2,1)S(1)} copy-done((bf16[32,1,1,1024]{3,0,2,1:T(8,128)(2,1)S(1)}, bf16[32,1,1,1024]{3,0,2,1:T(8,128)(2,1)}, u32[]{:S(2)}) %copy-start.1) | copy-done | bytes 65560
  0.8 0.8 %copy-done.2 = bf16[32,1,1,1024]{3,0,2,1:T(8,128)(2,1)S(1)} copy-done((bf16[32,1,1,1024]{3,0,2,1:T(8,128)(2,1)S(1)}, bf16[32,1,1,1024]{3,0,2,1:T(8,128)(2,1)}, u32[]{:S(2)}) %copy-start.2) | copy-done | bytes 65560
  1.7 0.7 %copy-done.3 = bf16[128,64]{0,1:T(8,128)(2,1)S(1)} copy-done((bf16[128,64]{0,1:T(8,128)(2,1)S(1)}, bf16[128,64]{0,1:T(8,128)(2,1)}, u32[]{:S(2)}) %copy-start.3) | copy-done | bytes 16408
  2.4 0.7 %copy-done.4 = s32[1,1,1024]{2,1,0:T(1,128)S(1)} copy-done((s32[1,1,1024]{2,1,0:T(1,128)S(1)}, s32[1,1,1024]{2,1,0:T(1,128)}, u32[]{:S(2)}) %copy-start.4) | copy-done | bytes 4120
  3.1 0.7 %copy-done.5 = s32[1,1,4,128]{3,2,1,0:T(4,128)S(1)} copy-done((s32[1,1,4,128]{3,2,1,0:T(4,128)S(1)}, s32[1,1,4,128]{3,2,1,0:T(4,128)}, u32[]{:S(2)}) %copy-start.5) | copy-done | bytes 2072
  3.8 0.8 %gather.1 = (bf16[32,128]{1,0:T(8,128)(2,1)S(1)}, bf16[32,128]{1,0:T(8,128)(2,1)S(1)}, bf16[32,128]{1,0:T(8,128)(2,1)S(1)}, bf16[32,128]{1,0:T(8,128)(2,1)S(1)},...) custom-call(bf16[32,1024]{1,0:T(8,128)(2,1)S(1)} %bitcast.8, ...), custom_call_target="tpu_custom_call" | custom-call | flops 1000000 | bytes 153600 | tf_op jit(solution)/shard_map/gather/pallas_call | solution.py:189
  4.5 2.5 %collective-permute-start = (bf16[32,128]{1,0:T(8,128)(2,1)S(1)}, bf16[32,128]{1,0:T(8,128)(2,1)S(1)}, u32[]{:S(2)}, u32[]{:S(2)}) collective-permute-start(bf16[32,128]{1,0:T(8,128)(2,1)S(1)} %get-tuple-element.32), channel_id=1, source_target_pairs={{0,24},{8,16},{16,8},{24,0},{1,25},{9,17},{17,9},{25,1},{2,26},{10... | collective-permute-start | bytes 24584 | tf_op jit(solution)/shard_map/ppermute | solution.py:230
  7.0 0.7 %collective-permute-start.1 = (bf16[32,128]{1,0:T(8,128)(2,1)S(1)}, bf16[32,128]{1,0:T(8,128)(2,1)S(1)}, u32[]{:S(2)}, u32[]{:S(2)}) collective-permute-start(bf16[32,128]{1,0:T(8,128)(2,1)S(1)} %get-tuple-element.33), channel_id=1, source_target_pairs={{0,8},{8,0},{16,24},{24,16},{1,9},{9,1},{17,25},{25,17},{2,10},{10... | collective-permute-start | bytes 24584 | tf_op jit(solution)/shard_map/ppermute | solution.py:232
  7.7 3.6 %collective-permute-start.2 = (bf16[32,128]{1,0:T(8,128)(2,1)S(1)}, bf16[32,128]{1,0:T(8,128)(2,1)S(1)}, u32[]{:S(2)}, u32[]{:S(2)}) collective-permute-start(bf16[32,128]{1,0:T(8,128)(2,1)S(1)} %get-tuple-element.34), channel_id=1, source_target_pairs={{0,6},{2,4},{4,2},{6,0},{1,7},{3,5},{5,3},{7,1},{8,14},{10,12},{12... | collective-permute-start | bytes 24584 | tf_op jit(solution)/shard_map/ppermute | solution.py:229
  11.3 1.5 %collective-permute-start.4 = (bf16[64,128]{1,0:T(8,128)(2,1)S(1)}, bf16[64,128]{1,0:T(8,128)(2,1)S(1)}, u32[]{:S(2)}, u32[]{:S(2)}) collective-permute-start(bf16[64,128]{1,0:T(8,128)(2,1)S(1)} %get-tuple-element.39.refs_0_), channel_id=1, source_target_pairs={{0,1},{1,0},{2,3},{3,2},{4,5},{5,4},{6,7},{7,6},{8,9},{9,8},{10,11... | collective-permute-start | bytes 49160 | tf_op jit(solution)/shard_map/ppermute | solution.py:233
  12.8 0.8 %pad_convert_fusion = f32[2560]{0:T(1024)S(1)} fusion(bf16[2559]{0:T(1024)(128)(2,1)} %param.9), kind=kLoop, calls=%fused_computation | loop fusion | flops 2560 | bytes 15358 | tf_op jit(solution)/shard_map/broadcast_in_dim | solution.py:236
  13.6 0.0 copy-start
  13.6 1.9 %copy-done = bf16[1,1,1024,1536]{3,2,1,0:T(8,128)(2,1)S(1)} copy-done((bf16[1,1,1024,1536]{3,2,1,0:T(8,128)(2,1)S(1)}, bf16[1,1,1024,1536]{3,2,1,0:T(8,128)(2,1)}, u32[]{:S(2)}) %copy-start) | copy-done | bytes 3145752
  15.5 1.2 %strip.1 = (bf16[256,2304]{1,0:T(8,128)(2,1)S(1)}, f32[32,1024]{1,0:T(8,128)S(1)}, bf16[1024,1536]{1,0:T(8,128)(2,1)S(1)}) custom-call(f32[1,2560]{1,0:T(1,128)S(1)} %reshape.kernel_ref, bf16[32,1024]{1,0:T(8,128)(2,1)S(1)} %get-tuple-element.29.own_ref, bf16[32,1024]{1,0:T(8,128)(2,1)S(1)} %get-tuple-element.30.right_ref, bf16[1024,1536]{1,0:T(8,128)(2,1)S(1)} %bitcast.7), custom_call_target="tpu_custom_call" | custom-call | flops 1000000 | bytes 3287040 | tf_op jit(solution)/shard_map/strip/pallas_call | solution.py:189
  16.7 0.1 columns.1
  16.7 0.0 collective-permute-done.1.ti
  16.8 0.0 collective-permute-done.2.uo
  16.8 0.7 %residual.1 = (bf16[64,128]{1,0:T(8,128)(2,1)S(1)}, bf16[32,128]{1,0:T(8,128)(2,1)S(1)}, bf16[64,128]{1,0:T(8,128)(2,1)S(1)}, bf16[32,128]{1,0:T(8,128)(2,1)S(1)...) custom-call(f32[32,1024]{1,0:T(8,128)S(1)} %get-tuple-element.31.base_ref, ...), custom_call_target="tpu_custom_call" | custom-call | flops 1000000 | bytes 4751360 | tf_op jit(solution)/shard_map/residual/pallas_call | solution.py:189
  17.5 0.0 collective-permute-start.5
  17.6 0.6 %collective-permute-start.6 = (bf16[64,128]{1,0:T(8,128)(2,1)S(1)}, bf16[64,128]{1,0:T(8,128)(2,1)S(1)}, u32[]{:S(2)}, u32[]{:S(2)}) collective-permute-start(bf16[64,128]{1,0:T(8,128)(2,1)S(1)} %get-tuple-element.44), channel_id=1, source_target_pairs={{0,8},{8,0},{16,24},{24,16},{1,9},{9,1},{17,25},{25,17},{2,10},{10... | collective-permute-start | bytes 49160 | tf_op jit(solution)/shard_map/ppermute | solution.py:270
  18.2 1.5 %collective-permute-start.7 = (bf16[32,128]{1,0:T(8,128)(2,1)S(1)}, bf16[32,128]{1,0:T(8,128)(2,1)S(1)}, u32[]{:S(2)}, u32[]{:S(2)}) collective-permute-start(bf16[32,128]{1,0:T(8,128)(2,1)S(1)} %get-tuple-element.48.refs_0_), channel_id=1, source_target_pairs={{0,16},{8,24},{16,0},{24,8},{1,17},{9,25},{17,1},{25,9},{2,18},{10... | collective-permute-start | bytes 24584 | tf_op jit(solution)/shard_map/ppermute | solution.py:269
  19.7 2.1 %collective-permute-done.7.refs_3_ = bf16[32,128]{1,0:T(8,128)(2,1)S(1)} collective-permute-done((bf16[32,128]{1,0:T(8,128)(2,1)S(1)}, bf16[32,128]{1,0:T(8,128)(2,1)S(1)}, u32[]{:S(2)}, u32[]{:S(2)}) %collective-permute-start.7) | collective-permute-done | bytes 8224 | tf_op jit(solution)/shard_map/ppermute | solution.py:269
  21.8 0.0 collective-permute-done.5.ro.refs_1_
  21.8 0.0 collective-permute-done.6.ri.refs_2_
  21.8 0.2 partial.1
  22.0 0.9 %collective-permute-start.8 = (f32[64,128]{1,0:T(8,128)S(1)}, f32[64,128]{1,0:T(8,128)S(1)}, u32[]{:S(2)}, u32[]{:S(2)}) collective-permute-start(f32[64,128]{1,0:T(8,128)S(1)} %get-tuple-element.50), channel_id=1, source_target_pairs={{0,6},{2,4},{4,2},{6,0},{1,7},{3,5},{5,3},{7,1},{8,14},{10,12},{12... | collective-permute-start | bytes 98312 | tf_op jit(solution)/shard_map/ppermute | solution.py:284
  23.0 1.2 %collective-permute-start.9 = (f32[64,128]{1,0:T(8,128)S(1)}, f32[64,128]{1,0:T(8,128)S(1)}, u32[]{:S(2)}, u32[]{:S(2)}) collective-permute-start(f32[64,128]{1,0:T(8,128)S(1)} %get-tuple-element.51), channel_id=1, source_target_pairs={{0,2},{2,0},{4,6},{6,4},{1,3},{3,1},{5,7},{7,5},{8,10},{10,8},{12,... | collective-permute-start | bytes 98312 | tf_op jit(solution)/shard_map/ppermute | solution.py:286
  24.1 2.3 %collective-permute-start.10 = (f32[32,128]{1,0:T(8,128)S(1)}, f32[32,128]{1,0:T(8,128)S(1)}, u32[]{:S(2)}, u32[]{:S(2)}) collective-permute-start(f32[32,128]{1,0:T(8,128)S(1)} %get-tuple-element.52), channel_id=1, source_target_pairs={{0,4},{2,6},{4,0},{6,2},{1,5},{3,7},{5,1},{7,3},{8,12},{10,14},{12... | collective-permute-start | bytes 49160 | tf_op jit(solution)/shard_map/ppermute | solution.py:285
  26.5 0.6 %local.1.acc_ref = f32[32,1024]{1,0:T(8,128)S(1)} custom-call(bf16[32,1024]{1,0:T(8,128)(2,1)S(1)} %get-tuple-element.41.res_ref, bf16[1024,1536]{1,0:T(8,128)(2,1)S(1)} %get-tuple-element.37.inv_ref, bf16[1024,512]{1,0:T(8,128)(2,1)S(1)} %get-tuple-element.42.spots_ref, bf16[64,128]{1,0:T(8,128)(2,1)S(1)} %collective-permute-done.5.ro.refs_1_, ...), custom_call_target="tpu_custom_call" | custom-call | flops 1000000 | bytes 4292608 | tf_op jit(solution)/shard_map/local/pallas_call | solution.py:189
  27.1 1.7 %collective-permute-done.10.refs_3_ = f32[32,128]{1,0:T(8,128)S(1)} collective-permute-done((f32[32,128]{1,0:T(8,128)S(1)}, f32[32,128]{1,0:T(8,128)S(1)}, u32[]{:S(2)}, u32[]{:S(2)}) %collective-permute-start.10) | collective-permute-done | bytes 16416 | tf_op jit(solution)/shard_map/ppermute | solution.py:285
  28.8 0.0 collective-permute-done.8.refs_1_
  28.8 1.0 %final.1 = bf16[32,1024]{1,0:T(8,128)(2,1)} custom-call(f32[32,1024]{1,0:T(8,128)S(1)} %local.1.acc_ref, bf16[128,1024]{1,0:T(8,128)(2,1)S(1)} %get-tuple-element.40.member_ref, bf16[1024,512]{1,0:T(8,128)(2,1)S(1)} %get-tuple-element.42.spots_ref, f32[32,128]{1,0:T(8,128)S(1)} %get-tuple-element.49.refs_0_, f32[64,128]{1,0:T(8,128)S(1)} %collective-permute-done.8.refs_1_, ...), custom_call_target="tpu_custom_call" | custom-call | flops 1000000 | bytes 1540096 | tf_op jit(solution)/shard_map/final/pallas_call | solution.py:189
  (11 shorter events, 0.0 us)
Async XLA Ops:
  0.0 0.8 %copy-start.1 = (bf16[32,1,1,1024]{3,0,2,1:T(8,128)(2,1)S(1)}, bf16[32,1,1,1024]{3,0,2,1:T(8,128)(2,1)}, u32[]{:S(2)}) copy-start(bf16[32,1,1,1024]{3,0,2,1:T(8,128)(2,1)} %param.7) | copy-start | bytes 196612
  0.8 0.8 %copy-start.2 = (bf16[32,1,1,1024]{3,0,2,1:T(8,128)(2,1)S(1)}, bf16[32,1,1,1024]{3,0,2,1:T(8,128)(2,1)}, u32[]{:S(2)}) copy-start(bf16[32,1,1,1024]{3,0,2,1:T(8,128)(2,1)} %param.8) | copy-start | bytes 196612
  1.7 0.7 %copy-start.3 = (bf16[128,64]{0,1:T(8,128)(2,1)S(1)}, bf16[128,64]{0,1:T(8,128)(2,1)}, u32[]{:S(2)}) copy-start(bf16[128,64]{0,1:T(8,128)(2,1)} %param.11) | copy-start | bytes 49156
  2.4 0.7 %copy-start.4 = (s32[1,1,1024]{2,1,0:T(1,128)S(1)}, s32[1,1,1024]{2,1,0:T(1,128)}, u32[]{:S(2)}) copy-start(s32[1,1,1024]{2,1,0:T(1,128)} %param.12) | copy-start | bytes 12292
  3.1 0.7 %copy-start.5 = (s32[1,1,4,128]{3,2,1,0:T(4,128)S(1)}, s32[1,1,4,128]{3,2,1,0:T(4,128)}, u32[]{:S(2)}) copy-start(s32[1,1,4,128]{3,2,1,0:T(4,128)} %param.13) | copy-start | bytes 6148
  4.5 12.2 %collective-permute-start = (bf16[32,128]{1,0:T(8,128)(2,1)S(1)}, bf16[32,128]{1,0:T(8,128)(2,1)S(1)}, u32[]{:S(2)}, u32[]{:S(2)}) collective-permute-start(bf16[32,128]{1,0:T(8,128)(2,1)S(1)} %get-tuple-element.32), channel_id=1, source_target_pairs={{0,24},{8,16},{16,8},{24,0},{1,25},{9,17},{17,9},{25,1},{2,26},{10... | collective-permute-start | bytes 24584 | tf_op jit(solution)/shard_map/ppermute | solution.py:230
  7.0 9.7 %collective-permute-start.1 = (bf16[32,128]{1,0:T(8,128)(2,1)S(1)}, bf16[32,128]{1,0:T(8,128)(2,1)S(1)}, u32[]{:S(2)}, u32[]{:S(2)}) collective-permute-start(bf16[32,128]{1,0:T(8,128)(2,1)S(1)} %get-tuple-element.33), channel_id=1, source_target_pairs={{0,8},{8,0},{16,24},{24,16},{1,9},{9,1},{17,25},{25,17},{2,10},{10... | collective-permute-start | bytes 24584 | tf_op jit(solution)/shard_map/ppermute | solution.py:232
  7.7 9.1 %collective-permute-start.2 = (bf16[32,128]{1,0:T(8,128)(2,1)S(1)}, bf16[32,128]{1,0:T(8,128)(2,1)S(1)}, u32[]{:S(2)}, u32[]{:S(2)}) collective-permute-start(bf16[32,128]{1,0:T(8,128)(2,1)S(1)} %get-tuple-element.34), channel_id=1, source_target_pairs={{0,6},{2,4},{4,2},{6,0},{1,7},{3,5},{5,3},{7,1},{8,14},{10,12},{12... | collective-permute-start | bytes 24584 | tf_op jit(solution)/shard_map/ppermute | solution.py:229
  11.3 5.5 %collective-permute-start.3 = (bf16[32,128]{1,0:T(8,128)(2,1)S(1)}, bf16[32,128]{1,0:T(8,128)(2,1)S(1)}, u32[]{:S(2)}, u32[]{:S(2)}) collective-permute-start(bf16[32,128]{1,0:T(8,128)(2,1)S(1)} %get-tuple-element.35), channel_id=1, source_target_pairs={{0,2},{2,0},{4,6},{6,4},{1,3},{3,1},{5,7},{7,5},{8,10},{10,8},{12,... | collective-permute-start | bytes 24584 | tf_op jit(solution)/shard_map/ppermute | solution.py:231
  11.3 5.4 %collective-permute-start.4 = (bf16[64,128]{1,0:T(8,128)(2,1)S(1)}, bf16[64,128]{1,0:T(8,128)(2,1)S(1)}, u32[]{:S(2)}, u32[]{:S(2)}) collective-permute-start(bf16[64,128]{1,0:T(8,128)(2,1)S(1)} %get-tuple-element.39.refs_0_), channel_id=1, source_target_pairs={{0,1},{1,0},{2,3},{3,2},{4,5},{5,4},{6,7},{7,6},{8,9},{9,8},{10,11... | collective-permute-start | bytes 49160 | tf_op jit(solution)/shard_map/ppermute | solution.py:233
  13.6 1.9 %copy-start = (bf16[1,1,1024,1536]{3,2,1,0:T(8,128)(2,1)S(1)}, bf16[1,1,1024,1536]{3,2,1,0:T(8,128)(2,1)}, u32[]{:S(2)}) copy-start(bf16[1,1,1024,1536]{3,2,1,0:T(8,128)(2,1)} %param.10) | copy-start | bytes 9437188
  17.5 4.3 %collective-permute-start.5 = (bf16[64,128]{1,0:T(8,128)(2,1)S(1)}, bf16[64,128]{1,0:T(8,128)(2,1)S(1)}, u32[]{:S(2)}, u32[]{:S(2)}) collective-permute-start(bf16[64,128]{1,0:T(8,128)(2,1)S(1)} %get-tuple-element.43), channel_id=1, source_target_pairs={{0,24},{8,16},{16,8},{24,0},{1,25},{9,17},{17,9},{25,1},{2,26},{10... | collective-permute-start | bytes 49160 | tf_op jit(solution)/shard_map/ppermute | solution.py:268
  17.6 4.3 %collective-permute-start.6 = (bf16[64,128]{1,0:T(8,128)(2,1)S(1)}, bf16[64,128]{1,0:T(8,128)(2,1)S(1)}, u32[]{:S(2)}, u32[]{:S(2)}) collective-permute-start(bf16[64,128]{1,0:T(8,128)(2,1)S(1)} %get-tuple-element.44), channel_id=1, source_target_pairs={{0,8},{8,0},{16,24},{24,16},{1,9},{9,1},{17,25},{25,17},{2,10},{10... | collective-permute-start | bytes 49160 | tf_op jit(solution)/shard_map/ppermute | solution.py:270
  18.2 3.7 %collective-permute-start.7 = (bf16[32,128]{1,0:T(8,128)(2,1)S(1)}, bf16[32,128]{1,0:T(8,128)(2,1)S(1)}, u32[]{:S(2)}, u32[]{:S(2)}) collective-permute-start(bf16[32,128]{1,0:T(8,128)(2,1)S(1)} %get-tuple-element.48.refs_0_), channel_id=1, source_target_pairs={{0,16},{8,24},{16,0},{24,8},{1,17},{9,25},{17,1},{25,9},{2,18},{10... | collective-permute-start | bytes 24584 | tf_op jit(solution)/shard_map/ppermute | solution.py:269
  22.0 6.7 %collective-permute-start.8 = (f32[64,128]{1,0:T(8,128)S(1)}, f32[64,128]{1,0:T(8,128)S(1)}, u32[]{:S(2)}, u32[]{:S(2)}) collective-permute-start(f32[64,128]{1,0:T(8,128)S(1)} %get-tuple-element.50), channel_id=1, source_target_pairs={{0,6},{2,4},{4,2},{6,0},{1,7},{3,5},{5,3},{7,1},{8,14},{10,12},{12... | collective-permute-start | bytes 98312 | tf_op jit(solution)/shard_map/ppermute | solution.py:284
  23.0 5.8 %collective-permute-start.9 = (f32[64,128]{1,0:T(8,128)S(1)}, f32[64,128]{1,0:T(8,128)S(1)}, u32[]{:S(2)}, u32[]{:S(2)}) collective-permute-start(f32[64,128]{1,0:T(8,128)S(1)} %get-tuple-element.51), channel_id=1, source_target_pairs={{0,2},{2,0},{4,6},{6,4},{1,3},{3,1},{5,7},{7,5},{8,10},{10,8},{12,... | collective-permute-start | bytes 98312 | tf_op jit(solution)/shard_map/ppermute | solution.py:286
  24.1 4.6 %collective-permute-start.10 = (f32[32,128]{1,0:T(8,128)S(1)}, f32[32,128]{1,0:T(8,128)S(1)}, u32[]{:S(2)}, u32[]{:S(2)}) collective-permute-start(f32[32,128]{1,0:T(8,128)S(1)} %get-tuple-element.52), channel_id=1, source_target_pairs={{0,4},{2,6},{4,0},{6,2},{1,5},{3,7},{5,1},{7,3},{8,12},{10,14},{12... | collective-permute-start | bytes 49160 | tf_op jit(solution)/shard_map/ppermute | solution.py:285

commit v2 on v1

--- a/solution.py
+++ b/solution.py
@@ -7,6 +7,7 @@
 from jax.experimental.pallas import tpu as pltpu
 from jax.sharding import PartitionSpec as P
 
+
 LANES = 128
 BLOCK = 256
 VMEM = pl.BlockSpec(memory_space=pltpu.VMEM)
@@ -53,14 +54,11 @@
     return [(i, (i + step) % count) for i in range(count)]
 
 
-def gather_kernel(own_hbm, send_hbm, right_hbm, labels_hbm, columns_hbm, co, ro, ci, ri, spots_ref, own_ref, right_ref, labels_ref, columns_ref, send_ref, sems):
-    pairs = (
-        (send_hbm, send_ref),
-        (own_hbm, own_ref),
-        (right_hbm, right_ref),
-        (labels_hbm, labels_ref),
-        (columns_hbm, columns_ref),
-    )
+def gather_kernel(send_hbm, own_hbm, *refs):
+    rest = (len(refs) - 8) // 2
+    more_hbm, (co, ro, ci, ri, spots_ref, own_ref) = refs[:rest], refs[rest : rest + 6]
+    more, (send_ref, sems) = refs[rest + 6 : -2], refs[-2:]
+    pairs = zip((send_hbm, own_hbm, *more_hbm), (send_ref, own_ref, *more))
     copies = [pltpu.make_async_copy(a, b, sems.at[i]) for i, (a, b) in enumerate(pairs)]
     for copy in copies:
         copy.start()
@@ -82,11 +80,9 @@
         copy.wait()
 
 
-def strip_kernel(kernel_ref, own_ref, right_ref, inv_hbm, strip_ref, base_ref, inv_ref, sem):
-    copy = pltpu.make_async_copy(inv_hbm, inv_ref, sem)
-    copy.start()
+def strip_kernel(kernel_ref, own_ref, right_ref, labels_ref, strip_ref, base_ref, member_ref):
+    n_core = own_ref.shape[1]
     width = kernel_ref.shape[1]
-    n_core = own_ref.shape[1]
     rows = 16
     row = jnp.broadcast_to(kernel_ref[...], (rows, width))
     first = pltpu.roll(row, 0, 1, stride=1, stride_axis=0)
@@ -99,12 +95,12 @@
         here = slice(b * BLOCK, (b + 1) * BLOCK)
         field = mm_nt(own, strip_ref[:, start : start + n_core])
         base_ref[:, here] = right_ref[:, here].astype(F32) - own[:, here].astype(F32) - field
-    copy.wait()
-
-
-def columns_kernel(labels_ref, *refs):
-    n_dev = len(refs) - 2
-    parts, columns_ref, member_ref = refs[:n_dev], refs[n_dev], refs[n_dev + 1]
+    member_ref[...] = one_hot(labels_ref[...], member_ref.shape[0])
+
+
+def columns_kernel(*refs):
+    parts, columns_ref = refs[:-1], refs[-1]
+    n_dev = len(parts)
     targets = partners("col")
     half = parts[0].shape[0] // len(targets)
     dev = lax.axis_index("dev")
@@ -114,10 +110,9 @@
         for e in range(n_dev):
             target = pl.multiple_of(lax.rem(dev + e, n_dev) * half, half)
             columns_ref[d, pl.ds(target, half), :] = parts[e][pl.ds(source, half), :]
-    member_ref[...] = one_hot(labels_ref[...], member_ref.shape[0])
-
-
-def residual_kernel(base_ref, to, ti, uo, ui, strip_ref, inv_ref, member_ref, ro, rx, ri, co, ci, res_ref):
+
+
+def residual_kernel(unknowns, base_ref, to, ti, uo, ui, strip_ref, inv_ref, member_ref, ro, rx, ri, co, ci, res_ref):
     n_core = base_ref.shape[1]
     rows, shell = to.shape
     odd_row, odd_col = place("row")[1] == 1, place("col")[1] == 1
@@ -131,7 +126,7 @@
         field = mm_nt(shells, strip_ref[:, start : start + width])
         res_ref[:, here] = (base_ref[:, here] - field).astype(BF16)
     res = res_ref[...]
-    coarse = mm_nt(res, member_ref[...]).astype(BF16)
+    coarse = pack(mm_nt(res, member_ref[...]), unknowns).astype(BF16)
     rx[...] = coarse
     local = mm(res, inv_ref[:, n_core:]).astype(BF16)
     back = [local[:, j * shell : (j + 1) * shell] for j in range(4)]
@@ -143,23 +138,30 @@
     ci[...] = jnp.where(odd_col, back[2], back[3])
 
 
-def partial_kernel(columns_ref, co, ci, *refs):
+def partial_kernel(unknowns, columns_ref, co, ci, *refs):
     sources = partners("row")
     n_bx = len(sources)
     gathered, outs = refs[:n_bx], refs[n_bx:]
     width = columns_ref.shape[2]
     rows = co.shape[0]
+    height = gathered[0].shape[0]
     total = jnp.zeros((rows, width), F32)
     for bx, ref in zip(sources, gathered):
-        piece = ref[-rows:, :].astype(F32)
+        piece = unpack(ref[-height:, :].astype(F32), unknowns)
         if width > LANES:
             piece = jnp.concatenate([piece, jnp.zeros((rows, width - LANES), F32)], axis=1)
-        total = total + pltpu.roll(piece, bx * (width // n_bx), 1)
+        total = total + pltpu.roll(piece, bx * unknowns, 1)
     total = total.astype(BF16)
-    outs[1][:rows, :] = co[...].astype(F32)
-    outs[2][:rows, :] = ci[...].astype(F32)
+    outs[1][:rows, :] = co[...]
+    outs[2][:rows, :] = ci[...]
     for d, out in enumerate(outs):
-        out[-rows:, :] = mm_nt(total, columns_ref[d])
+        part = pack(mm_nt(total, columns_ref[d]), unknowns)
+        if d == 0:
+            out[...] = part
+        else:
+            high = part.astype(BF16)
+            out[-2 * height : -height, :] = high
+            out[-height:, :] = (part - high.astype(F32)).astype(BF16)
 
 
 def local_kernel(res_ref, inv_ref, spots_ref, ro, ri, acc_ref):
@@ -169,22 +171,38 @@
     acc_ref[...] = mm(res_ref[...], inv_ref[:, :n_core]).astype(BF16).astype(F32) + added
 
 
-def final_kernel(acc_ref, member_ref, spots_ref, *refs):
+def final_kernel(unknowns, acc_ref, member_ref, spots_ref, *refs):
     parts, out_ref = refs[:-1], refs[-1]
     rows = acc_ref.shape[0]
+    height = parts[0].shape[0]
     solved = parts[0][...]
     for part in parts[1:]:
-        solved = solved + part[-rows:, :]
+        solved = solved + part[-2 * height : -height, :].astype(F32) + part[-height:, :].astype(F32)
+    solved = unpack(solved, unknowns)
     high = solved.astype(BF16)
     low = (solved - high.astype(F32)).astype(BF16)
     both = mm(jnp.concatenate([high, low], axis=0), member_ref[...])
-    arrived = jnp.concatenate([parts[1][:rows, :], parts[2][:rows, :]], axis=1).astype(BF16)
+    arrived = jnp.concatenate([parts[1][:rows, :], parts[2][:rows, :]], axis=1)
     added = mm_nt(arrived, spots_ref[:, arrived.shape[1] :])
     out_ref[...] = (acc_ref[...] + added + both[:rows] + both[rows:]).astype(BF16)
 
 
-def call(body, name, shapes, *args, hbm=(), scratch=(), limit=16, flops=10**6):
+def pack(value, unknowns):
+    groups = LANES // unknowns
+    height = value.shape[0] // groups
+    parts = [pltpu.roll(value[q * height : (q + 1) * height, :], q * unknowns, 1) for q in range(1, groups)]
+    return sum(parts, value[:height, :])
+
+
+def unpack(packed, unknowns):
+    keep = lax.broadcasted_iota(jnp.int32, packed.shape, 1) < unknowns
+    parts = [packed] + [pltpu.roll(packed, LANES - q * unknowns, 1) for q in range(1, LANES // unknowns)]
+    return jnp.concatenate([jnp.where(keep, part, 0.0) for part in parts], axis=0)
+
+
+def call(body, shapes, *args, hbm=(), scratch=(), limit=16, flops=10**6):
     out_shape = [jax.ShapeDtypeStruct(s, t) for s, t in shapes]
+    args = [pltpu.with_memory_space_constraint(a, pltpu.HBM) if i in hbm else a for i, a in enumerate(args)]
     size = sum(a.size * a.dtype.itemsize for a in args)
     return pl.pallas_call(
         body,
@@ -192,7 +210,6 @@
         in_specs=[HBM if i in hbm else VMEM for i in range(len(args))],
         out_specs=[VMEM] * len(out_shape),
         scratch_shapes=scratch,
-        name=name,
         compiler_params=pltpu.CompilerParams(vmem_limit_bytes=limit << 20),
         cost_estimate=pl.CostEstimate(flops=flops, bytes_accessed=size, transcendentals=0),
     )(*args)
@@ -211,20 +228,19 @@
     n_bx, n_by, n_dev = (lax.axis_size(a) for a in ("row", "col", "dev"))
     coarse_rows = coarse_inverse.shape[0]
     shell = ((rows, n_shell), BF16)
-    double = ((2 * rows, LANES), BF16)
-
-    same = [(a.shape, a.dtype) for a in (own, right, labels, mine)]
-    co, ro, ci, ri, spots, own, right, labels, mine = call(
+    unknowns = coarse_rows // n_bx
+    height = rows * unknowns // LANES
+    double = ((rows + height, LANES), BF16)
+
+    held = (own, right, labels, mine, kernel)
+    co, ro, ci, ri, spots, own, right, labels, mine, kernel = call(
         gather_kernel,
-        "gather",
-        [shell] * 4 + [((n_core, 4 * n_shell), BF16)] + same,
-        own,
+        [shell] * 4 + [((n_core, 4 * n_shell), BF16)] + [(a.shape, a.dtype) for a in held],
         send,
-        right,
-        labels,
-        mine,
-        hbm=range(5),
-        scratch=[pltpu.VMEM(send.shape, send.dtype), pltpu.SemaphoreType.DMA((5,))],
+        *held,
+        hbm=range(6),
+        flops=4 * 10**9,
+        scratch=[pltpu.VMEM(send.shape, send.dtype), pltpu.SemaphoreType.DMA((6,))],
     )
     uo = lax.ppermute(co, "col", outer_pairs(n_by))
     to = lax.ppermute(ro, "row", outer_pairs(n_bx))
@@ -234,28 +250,17 @@
 
     width = n_core + n_patch
     padded = jnp.pad(kernel.astype(F32), (1, width - kernel.shape[0] - 1))[None, :]
-    strip, base, inverse = call(
+    strip, base, member = call(
         strip_kernel,
-        "strip",
-        [((BLOCK, width - BLOCK), BF16), ((rows, n_core), F32), (inverse.shape, BF16)],
+        [((BLOCK, width - BLOCK), BF16), ((rows, n_core), F32), ((LANES, n_core), BF16)],
         padded,
         own,
         right,
-        inverse,
-        hbm=(3,),
-        scratch=[pltpu.SemaphoreType.DMA],
-    )
-    columns, member = call(
-        columns_kernel,
-        "columns",
-        [((n_by, LANES, coarse_rows), BF16), ((LANES, n_core), BF16)],
         labels,
-        *halves,
     )
     ro, rx, ri, co, ci, res = call(
-        residual_kernel,
-        "residual",
-        [double, shell, double, shell, shell, ((rows, n_core), BF16)],
+        functools.partial(residual_kernel, unknowns),
+        [double, ((height, LANES), BF16), double, shell, shell, ((rows, n_core), BF16)],
         base,
         to,
         ti,
@@ -268,11 +273,11 @@
     ao = lax.ppermute(ro, "row", outer_pairs(n_bx))
     rest = [lax.ppermute(rx, "row", shifted(n_bx, -o)) for o in range(2, n_bx - 1)]
     ai = lax.ppermute(ri, "row", inner_pairs(n_bx))
-    single, wide = ((rows, LANES), F32), ((2 * rows, LANES), F32)
+    (columns,) = call(columns_kernel, [((n_by, LANES, coarse_rows), BF16)], *halves)
+    single, wide = ((2 * height, LANES), BF16), ((rows + 2 * height, LANES), BF16)
     partials = call(
-        partial_kernel,
-        "partial",
-        [single, wide, wide] + [single] * (n_by - 3),
+        functools.partial(partial_kernel, unknowns),
+        [((height, LANES), F32), wide, wide] + [single] * (n_by - 3),
         columns,
         co,
         ci,
@@ -284,8 +289,8 @@
     so = lax.ppermute(partials[1], "col", outer_pairs(n_by))
     others = [lax.ppermute(partials[d + 1], "col", shifted(n_by, d)) for d in range(2, n_by - 1)]
     si = lax.ppermute(partials[2], "col", inner_pairs(n_by))
-    (acc,) = call(local_kernel, "local", [((rows, n_core), F32)], res, inverse, spots, ao, ai)
-    (out,) = call(final_kernel, "final", [((rows, n_core), BF16)], acc, member, spots, partials[0], so, si, *others)
+    (acc,) = call(local_kernel, [((rows, n_core), F32)], res, inverse, spots, ao, ai)
+    (out,) = call(functools.partial(final_kernel, unknowns), [((rows, n_core), BF16)], acc, member, spots, partials[0], so, si, *others)
     return out[:, None, None, :]
 
 
@@ -300,6 +305,5 @@
         P("row", "col", None, None),
     )
     out_specs = P("dev", "row", "col", None)
-    return jax.shard_map(
-        per_device, mesh=mesh, in_specs=in_specs, out_specs=out_specs, check_vma=False
-    )
+
+    return jax.shard_map(per_device, mesh=mesh, in_specs=in_specs, out_specs=out_specs, check_vma=False)

time: 30.1 us -> 24.7 us (0.82)
  local copies, waits for them, and re-layouts: 5.66 us -> 0.01 us
  other arithmetic: 0.76 us -> 0.07 us
  Pallas kernels: 4.52 us -> 5.13 us
  waiting for transfers between devices: 3.83 us -> 4.41 us
    unnamed x12 -> x2, local copies, waits for them, and re-layouts: 5.65 us -> 0.01 us
    ppermute x1, starting transfers between devices: 1.15 us -> 0.01 us  [per_device(): si = lax.ppermute(partials[2], 'col', inner_pairs(n_by))]
    ppermute x1, waiting for transfers between devices: 0.01 us -> 1.06 us  [per_device(): ui = lax.ppermute(ci, 'col', inner_pairs(n_by))]
    ppermute x1, starting transfers between devices: 0.92 us -> 1.87 us  [per_device(): so = lax.ppermute(partials[1], 'col', outer_pairs(n_by))]
    broadcast_in_dim x1, other arithmetic: 0.76 us -> 0.07 us  [per_device(): jnp.pad(kernel.astype(F32), (1, width - kernel.shape[0] - 1))[None, :]]
    pallas_call x7, Pallas kernels: 4.52 us -> 5.13 us  [call(): pl.pallas_call(body, out_shape=out_shape, in_specs=[HBM if i in hbm else...]
    ppermute x1, waiting for transfers between devices: 1.67 us -> 1.29 us  [per_device(): lax.ppermute(partials[d + 1], 'col', shifted(n_by, d))]
  transfers between devices with their start and end apart: 11 -> 11, of which waited for: 2 -> 3; matrix products, arithmetic and copies ran while one was open for 3% -> 0% of each run, Pallas kernels for 6% -> 10%
where the time goes in v2:
time: 24.7 us; the launch traced here: 24.6 us
  starting transfers between devices  14.9 us (60%)
  Pallas kernels  5.13 us (21%)
  waiting for transfers between devices  4.41 us (18%)
    pallas_call x7, Pallas kernels, call(): pl.pallas_call(body, out_shape=out_shape, in_specs=[HBM if i in hbm else...  5.13 us
    ppermute x1, starting transfers between devices, per_device(): uo = lax.ppermute(co, 'col', outer_pairs(n_by))  3.6 us
    ppermute x1, starting transfers between devices, per_device(): lax.ppermute(partials[d + 1], 'col', shifted(n_by, d))  2.58 us
    ppermute x1, starting transfers between devices, per_device(): to = lax.ppermute(ro, 'row', outer_pairs(n_bx))  2.5 us
    ppermute x1, waiting for transfers between devices, per_device(): lax.ppermute(rx, 'row', shifted(n_bx, -o))  2.03 us
    ppermute x1, starting transfers between devices, per_device(): so = lax.ppermute(partials[1], 'col', outer_pairs(n_by))  1.87 us
    ppermute x1, starting transfers between devices, per_device(): lax.ppermute(rx, 'row', shifted(n_bx, -o))  1.52 us
    ppermute x1, starting transfers between devices, per_device(): lax.ppermute(mine, 'dev', shifted(n_dev, -e))  1.49 us
  transfers between devices with their start and end apart: 11, of which 3 were waited for; matrix products, arithmetic and copies ran while one was open for 0% of the time, Pallas kernels for 10%

profile of v2, /device:TPU:0, one launch (start us, length us, event | category | flops | bytes accessed | tf_op | source)
XLA Modules:
  0.0 24.6 jit_solution(3169401902707715168)
XLA Ops:
  0.0 0.0 copy-start
  0.0 1.4 %shard_map.73 = (bf16[32,128]{1,0:T(8,128)(2,1)S(1)}, bf16[32,128]{1,0:T(8,128)(2,1)S(1)}, bf16[32,128]{1,0:T(8,128)(2,1)S(1)}, bf16[32,128]{1,0:T(8,128)(2,1)S(...) custom-call(s32[4,128]{1,0:T(4,128)} %bitcast.13, ...), custom_call_target="tpu_custom_call" | custom-call | flops 4000000000 | bytes 158718 | tf_op jit(solution)/shard_map/pallas_call | solution.py:207
  1.4 2.5 %collective-permute-start = (bf16[32,128]{1,0:T(8,128)(2,1)S(1)}, bf16[32,128]{1,0:T(8,128)(2,1)S(1)}, u32[]{:S(2)}, u32[]{:S(2)}) collective-permute-start(bf16[32,128]{1,0:T(8,128)(2,1)S(1)} %get-tuple-element.33), channel_id=1, source_target_pairs={{0,24},{8,16},{16,8},{24,0},{1,25},{9,17},{17,9},{25,1},{2,26},{10... | collective-permute-start | bytes 24584 | tf_op jit(solution)/shard_map/ppermute | solution.py:246
  3.9 0.7 %collective-permute-start.1 = (bf16[32,128]{1,0:T(8,128)(2,1)S(1)}, bf16[32,128]{1,0:T(8,128)(2,1)S(1)}, u32[]{:S(2)}, u32[]{:S(2)}) collective-permute-start(bf16[32,128]{1,0:T(8,128)(2,1)S(1)} %get-tuple-element.34), channel_id=1, source_target_pairs={{0,8},{8,0},{16,24},{24,16},{1,9},{9,1},{17,25},{25,17},{2,10},{10... | collective-permute-start | bytes 24584 | tf_op jit(solution)/shard_map/ppermute | solution.py:248
  4.6 3.6 %collective-permute-start.2 = (bf16[32,128]{1,0:T(8,128)(2,1)S(1)}, bf16[32,128]{1,0:T(8,128)(2,1)S(1)}, u32[]{:S(2)}, u32[]{:S(2)}) collective-permute-start(bf16[32,128]{1,0:T(8,128)(2,1)S(1)} %get-tuple-element.35), channel_id=1, source_target_pairs={{0,6},{2,4},{4,2},{6,0},{1,7},{3,5},{5,3},{7,1},{8,14},{10,12},{12... | collective-permute-start | bytes 24584 | tf_op jit(solution)/shard_map/ppermute | solution.py:245
  8.2 0.0 collective-permute-start.3
  8.2 1.5 %collective-permute-start.6 = (bf16[64,128]{1,0:T(8,128)(2,1)S(1)}, bf16[64,128]{1,0:T(8,128)(2,1)S(1)}, u32[]{:S(2)}, u32[]{:S(2)}) collective-permute-start(bf16[64,128]{1,0:T(8,128)(2,1)S(1)} %get-tuple-element.43.refs_0_), channel_id=1, source_target_pairs={{0,1},{1,0},{2,3},{3,2},{4,5},{5,4},{6,7},{7,6},{8,9},{9,8},{10,11... | collective-permute-start | bytes 49160 | tf_op jit(solution)/shard_map/ppermute | solution.py:249
  9.7 0.1 pad_convert_fusion
  9.8 1.0 %shard_map.74 = (bf16[256,2304]{1,0:T(8,128)(2,1)S(1)}, f32[32,1024]{1,0:T(8,128)S(1)}, bf16[128,1024]{1,0:T(8,128)(2,1)S(1)}) custom-call(f32[1,2560]{1,0:T(1,128)S(1)} %reshape.kernel_ref, bf16[32,1024]{1,0:T(8,128)(2,1)S(1)} %get-tuple-element.29.own_ref, bf16[32,1024]{1,0:T(8,128)(2,1)S(1)} %get-tuple-element.30.right_ref, ...), custom_call_target="tpu_custom_call" | custom-call | flops 1000000 | bytes 145408 | tf_op jit(solution)/shard_map/pallas_call | solution.py:207
  10.8 0.0 collective-permute-done.to
  10.8 0.0 collective-permute-done.1.ti
  10.8 0.0 collective-permute-done.2.uo
  10.8 1.1 %collective-permute-done.3.ui = bf16[32,128]{1,0:T(8,128)(2,1)S(1)} collective-permute-done((bf16[32,128]{1,0:T(8,128)(2,1)S(1)}, bf16[32,128]{1,0:T(8,128)(2,1)S(1)}, u32[]{:S(2)}, u32[]{:S(2)}) %collective-permute-start.3) | collective-permute-done | bytes 8224 | tf_op jit(solution)/shard_map/ppermute | solution.py:247
  11.9 0.0 copy-done
  11.9 0.7 %shard_map.75 = (bf16[40,128]{1,0:T(8,128)(2,1)S(1)}, bf16[8,128]{1,0:T(8,128)(2,1)S(1)}, bf16[40,128]{1,0:T(8,128)(2,1)S(1)}, bf16[32,128]{1,0:T(8,128)(2,1)S(1...) custom-call(f32[32,1024]{1,0:T(8,128)S(1)} %get-tuple-element.32.base_ref, ...), custom_call_target="tpu_custom_call" | custom-call | flops 1000000 | bytes 4751360 | tf_op jit(solution)/shard_map/pallas_call | solution.py:207
  12.6 0.0 collective-permute-start.4
  12.7 0.6 %collective-permute-start.5 = (bf16[40,128]{1,0:T(8,128)(2,1)S(1)}, bf16[40,128]{1,0:T(8,128)(2,1)S(1)}, u32[]{:S(2)}, u32[]{:S(2)}) collective-permute-start(bf16[40,128]{1,0:T(8,128)(2,1)S(1)} %get-tuple-element.42), channel_id=1, source_target_pairs={{0,8},{8,0},{16,24},{24,16},{1,9},{9,1},{17,25},{25,17},{2,10},{10... | collective-permute-start | bytes 30728 | tf_op jit(solution)/shard_map/ppermute | solution.py:275
  13.3 1.5 %collective-permute-start.7 = (bf16[8,128]{1,0:T(8,128)(2,1)S(1)}, bf16[8,128]{1,0:T(8,128)(2,1)S(1)}, u32[]{:S(2)}, u32[]{:S(2)}) collective-permute-start(bf16[8,128]{1,0:T(8,128)(2,1)S(1)} %get-tuple-element.46.refs_0_), channel_id=1, source_target_pairs={{0,16},{8,24},{16,0},{24,8},{1,17},{9,25},{17,1},{25,9},{2,18},{10... | collective-permute-start | bytes 6152 | tf_op jit(solution)/shard_map/ppermute | solution.py:274
  14.8 0.0 collective-permute-done.6.refs_1_
  14.8 2.0 %collective-permute-done.7.refs_3_ = bf16[8,128]{1,0:T(8,128)(2,1)S(1)} collective-permute-done((bf16[8,128]{1,0:T(8,128)(2,1)S(1)}, bf16[8,128]{1,0:T(8,128)(2,1)S(1)}, u32[]{:S(2)}, u32[]{:S(2)}) %collective-permute-start.7) | collective-permute-done | bytes 2080 | tf_op jit(solution)/shard_map/ppermute | solution.py:274
  16.9 0.0 collective-permute-done.4.ro.refs_1_
  16.9 0.0 collective-permute-done.5.ri.refs_2_
  16.9 0.3 %shard_map.78 = (f32[8,128]{1,0:T(8,128)S(1)}, bf16[48,128]{1,0:T(8,128)(2,1)S(1)}, bf16[48,128]{1,0:T(8,128)(2,1)S(1)}, bf16[16,128]{1,0:T(8,128)(2,1)S(1)}) custom-call(bf16[4,128,128]{2,1,0:T(8,128)(2,1)S(1)} %shard_map.77.columns_ref, bf16[32,128]{1,0:T(8,128)(2,1)S(1)} %get-tuple-element.44.co, bf16[32,128]{1,0:T(8,128)(2,1)S(1)} %get-tuple-element.45.ci, ...), custom_call_target="tpu_custom_call" | custom-call | flops 1000000 | bytes 172032 | tf_op jit(solution)/shard_map/pallas_call | solution.py:207
  17.2 1.9 %collective-permute-start.8 = (bf16[48,128]{1,0:T(8,128)(2,1)S(1)}, bf16[48,128]{1,0:T(8,128)(2,1)S(1)}, u32[]{:S(2)}, u32[]{:S(2)}) collective-permute-start(bf16[48,128]{1,0:T(8,128)(2,1)S(1)} %get-tuple-element.48), channel_id=1, source_target_pairs={{0,6},{2,4},{4,2},{6,0},{1,7},{3,5},{5,3},{7,1},{8,14},{10,12},{12... | collective-permute-start | bytes 36872 | tf_op jit(solution)/shard_map/ppermute | solution.py:289
  19.1 0.0 collective-permute-start.9
  19.1 2.6 %collective-permute-start.10 = (bf16[16,128]{1,0:T(8,128)(2,1)S(1)}, bf16[16,128]{1,0:T(8,128)(2,1)S(1)}, u32[]{:S(2)}, u32[]{:S(2)}) collective-permute-start(bf16[16,128]{1,0:T(8,128)(2,1)S(1)} %get-tuple-element.50), channel_id=1, source_target_pairs={{0,4},{2,6},{4,0},{6,2},{1,5},{3,7},{5,1},{7,3},{8,12},{10,14},{12... | collective-permute-start | bytes 12296 | tf_op jit(solution)/shard_map/ppermute | solution.py:290
  21.7 0.6 %shard_map.76.acc_ref = f32[32,1024]{1,0:T(8,128)S(1)} custom-call(bf16[32,1024]{1,0:T(8,128)(2,1)S(1)} %get-tuple-element.39.res_ref, bf16[1024,1536]{1,0:T(8,128)(2,1)S(1)} %bitcast.8, bf16[1024,512]{1,0:T(8,128)(2,1)S(1)} %get-tuple-element.40.spots_ref, bf16[40,128]{1,0:T(8,128)(2,1)S(1)} %collective-permute-done.4.ro.refs_1_, ...), custom_call_target="tpu_custom_call" | custom-call | flops 1000000 | bytes 4280320 | tf_op jit(solution)/shard_map/pallas_call | solution.py:207
  22.3 1.3 %collective-permute-done.10.refs_3_ = bf16[16,128]{1,0:T(8,128)(2,1)S(1)} collective-permute-done((bf16[16,128]{1,0:T(8,128)(2,1)S(1)}, bf16[16,128]{1,0:T(8,128)(2,1)S(1)}, u32[]{:S(2)}, u32[]{:S(2)}) %collective-permute-start.10) | collective-permute-done | bytes 4128 | tf_op jit(solution)/shard_map/ppermute | solution.py:290
  23.6 0.0 collective-permute-done.8.refs_1_
  23.6 0.0 collective-permute-done.9.refs_2_
  23.6 1.0 %shard_map.79 = bf16[32,1024]{1,0:T(8,128)(2,1)} custom-call(f32[32,1024]{1,0:T(8,128)S(1)} %shard_map.76.acc_ref, bf16[128,1024]{1,0:T(8,128)(2,1)S(1)} %get-tuple-element.38.member_ref, bf16[1024,512]{1,0:T(8,128)(2,1)S(1)} %get-tuple-element.40.spots_ref, f32[8,128]{1,0:T(8,128)S(1)} %get-tuple-element.47.refs_0_, ...), custom_call_target="tpu_custom_call" | custom-call | flops 1000000 | bytes 1474560 | tf_op jit(solution)/shard_map/pallas_call | solution.py:207
  (2 shorter events, 0.0 us)
Async XLA Ops:
  0.0 11.9 %copy-start = (bf16[1,1,1024,1536]{3,2,1,0:T(8,128)(2,1)S(1)}, bf16[1,1,1024,1536]{3,2,1,0:T(8,128)(2,1)}, u32[]{:S(2)}) copy-start(bf16[1,1,1024,1536]{3,2,1,0:T(8,128)(2,1)} %param.10) | copy-start | bytes 9437188
  1.4 9.3 %collective-permute-start = (bf16[32,128]{1,0:T(8,128)(2,1)S(1)}, bf16[32,128]{1,0:T(8,128)(2,1)S(1)}, u32[]{:S(2)}, u32[]{:S(2)}) collective-permute-start(bf16[32,128]{1,0:T(8,128)(2,1)S(1)} %get-tuple-element.33), channel_id=1, source_target_pairs={{0,24},{8,16},{16,8},{24,0},{1,25},{9,17},{17,9},{25,1},{2,26},{10... | collective-permute-start | bytes 24584 | tf_op jit(solution)/shard_map/ppermute | solution.py:246
  3.9 6.9 %collective-permute-start.1 = (bf16[32,128]{1,0:T(8,128)(2,1)S(1)}, bf16[32,128]{1,0:T(8,128)(2,1)S(1)}, u32[]{:S(2)}, u32[]{:S(2)}) collective-permute-start(bf16[32,128]{1,0:T(8,128)(2,1)S(1)} %get-tuple-element.34), channel_id=1, source_target_pairs={{0,8},{8,0},{16,24},{24,16},{1,9},{9,1},{17,25},{25,17},{2,10},{10... | collective-permute-start | bytes 24584 | tf_op jit(solution)/shard_map/ppermute | solution.py:248
  4.6 6.2 %collective-permute-start.2 = (bf16[32,128]{1,0:T(8,128)(2,1)S(1)}, bf16[32,128]{1,0:T(8,128)(2,1)S(1)}, u32[]{:S(2)}, u32[]{:S(2)}) collective-permute-start(bf16[32,128]{1,0:T(8,128)(2,1)S(1)} %get-tuple-element.35), channel_id=1, source_target_pairs={{0,6},{2,4},{4,2},{6,0},{1,7},{3,5},{5,3},{7,1},{8,14},{10,12},{12... | collective-permute-start | bytes 24584 | tf_op jit(solution)/shard_map/ppermute | solution.py:245
  8.2 3.7 %collective-permute-start.3 = (bf16[32,128]{1,0:T(8,128)(2,1)S(1)}, bf16[32,128]{1,0:T(8,128)(2,1)S(1)}, u32[]{:S(2)}, u32[]{:S(2)}) collective-permute-start(bf16[32,128]{1,0:T(8,128)(2,1)S(1)} %get-tuple-element.36), channel_id=1, source_target_pairs={{0,2},{2,0},{4,6},{6,4},{1,3},{3,1},{5,7},{7,5},{8,10},{10,8},{12,... | collective-permute-start | bytes 24584 | tf_op jit(solution)/shard_map/ppermute | solution.py:247
  8.2 6.6 %collective-permute-start.6 = (bf16[64,128]{1,0:T(8,128)(2,1)S(1)}, bf16[64,128]{1,0:T(8,128)(2,1)S(1)}, u32[]{:S(2)}, u32[]{:S(2)}) collective-permute-start(bf16[64,128]{1,0:T(8,128)(2,1)S(1)} %get-tuple-element.43.refs_0_), channel_id=1, source_target_pairs={{0,1},{1,0},{2,3},{3,2},{4,5},{5,4},{6,7},{7,6},{8,9},{9,8},{10,11... | collective-permute-start | bytes 49160 | tf_op jit(solution)/shard_map/ppermute | solution.py:249
  12.6 4.3 %collective-permute-start.4 = (bf16[40,128]{1,0:T(8,128)(2,1)S(1)}, bf16[40,128]{1,0:T(8,128)(2,1)S(1)}, u32[]{:S(2)}, u32[]{:S(2)}) collective-permute-start(bf16[40,128]{1,0:T(8,128)(2,1)S(1)} %get-tuple-element.41), channel_id=1, source_target_pairs={{0,24},{8,16},{16,8},{24,0},{1,25},{9,17},{17,9},{25,1},{2,26},{10... | collective-permute-start | bytes 30728 | tf_op jit(solution)/shard_map/ppermute | solution.py:273
  12.7 4.2 %collective-permute-start.5 = (bf16[40,128]{1,0:T(8,128)(2,1)S(1)}, bf16[40,128]{1,0:T(8,128)(2,1)S(1)}, u32[]{:S(2)}, u32[]{:S(2)}) collective-permute-start(bf16[40,128]{1,0:T(8,128)(2,1)S(1)} %get-tuple-element.42), channel_id=1, source_target_pairs={{0,8},{8,0},{16,24},{24,16},{1,9},{9,1},{17,25},{25,17},{2,10},{10... | collective-permute-start | bytes 30728 | tf_op jit(solution)/shard_map/ppermute | solution.py:275
  13.3 3.6 %collective-permute-start.7 = (bf16[8,128]{1,0:T(8,128)(2,1)S(1)}, bf16[8,128]{1,0:T(8,128)(2,1)S(1)}, u32[]{:S(2)}, u32[]{:S(2)}) collective-permute-start(bf16[8,128]{1,0:T(8,128)(2,1)S(1)} %get-tuple-element.46.refs_0_), channel_id=1, source_target_pairs={{0,16},{8,24},{16,0},{24,8},{1,17},{9,25},{17,1},{25,9},{2,18},{10... | collective-permute-start | bytes 6152 | tf_op jit(solution)/shard_map/ppermute | solution.py:274
  17.2 6.4 %collective-permute-start.8 = (bf16[48,128]{1,0:T(8,128)(2,1)S(1)}, bf16[48,128]{1,0:T(8,128)(2,1)S(1)}, u32[]{:S(2)}, u32[]{:S(2)}) collective-permute-start(bf16[48,128]{1,0:T(8,128)(2,1)S(1)} %get-tuple-element.48), channel_id=1, source_target_pairs={{0,6},{2,4},{4,2},{6,0},{1,7},{3,5},{5,3},{7,1},{8,14},{10,12},{12... | collective-permute-start | bytes 36872 | tf_op jit(solution)/shard_map/ppermute | solution.py:289
  19.1 4.5 %collective-permute-start.9 = (bf16[48,128]{1,0:T(8,128)(2,1)S(1)}, bf16[48,128]{1,0:T(8,128)(2,1)S(1)}, u32[]{:S(2)}, u32[]{:S(2)}) collective-permute-start(bf16[48,128]{1,0:T(8,128)(2,1)S(1)} %get-tuple-element.49), channel_id=1, source_target_pairs={{0,2},{2,0},{4,6},{6,4},{1,3},{3,1},{5,7},{7,5},{8,10},{10,8},{12,... | collective-permute-start | bytes 36872 | tf_op jit(solution)/shard_map/ppermute | solution.py:291
  19.1 4.5 %collective-permute-start.10 = (bf16[16,128]{1,0:T(8,128)(2,1)S(1)}, bf16[16,128]{1,0:T(8,128)(2,1)S(1)}, u32[]{:S(2)}, u32[]{:S(2)}) collective-permute-start(bf16[16,128]{1,0:T(8,128)(2,1)S(1)} %get-tuple-element.50), channel_id=1, source_target_pairs={{0,4},{2,6},{4,0},{6,2},{1,5},{3,7},{5,1},{7,3},{8,12},{10,14},{12... | collective-permute-start | bytes 12296 | tf_op jit(solution)/shard_map/ppermute | solution.py:290

commit v3 on v2

--- a/solution.py
+++ b/solution.py
@@ -26,8 +26,18 @@
 
 def one_hot(labels, rows):
     shape = (rows, labels.shape[1])
-    hit = lax.broadcasted_iota(jnp.int32, shape, 0) == jnp.broadcast_to(labels, shape)
-    return jnp.where(hit, 1.0, 0.0).astype(BF16)
+    hit = lax.broadcasted_iota(jnp.int16, shape, 0) == jnp.broadcast_to(labels.astype(jnp.int16), shape)
+    return jnp.where(hit, jnp.ones(shape, BF16), jnp.zeros(shape, BF16))
+
+
+def toeplitz(values, strip_ref, offset, blocks):
+    rows, parts = values.shape[0], values.shape[1] // BLOCK
+    stacked = jnp.concatenate([values[:, u * BLOCK : (u + 1) * BLOCK] for u in range(parts)], axis=0)
+    starts = [offset + BLOCK * t for t in range(blocks - 1 + parts)]
+    tiles = [mm_nt(stacked, strip_ref[:, start : start + BLOCK]) for start in starts]
+    return [
+        sum(tiles[blocks - 1 - b + u][u * rows : (u + 1) * rows] for u in range(parts)) for b in range(blocks)
+    ]
 
 
 def place(axis):
@@ -90,21 +100,22 @@
         part = first if g == 0 else pltpu.roll(first, g * rows, 1)
         strip_ref[g * rows : (g + 1) * rows, :] = part[:, BLOCK:].astype(BF16)
     own = own_ref[...]
-    for b in range(n_core // BLOCK):
-        start = n_core - BLOCK - BLOCK * b
+    for b, field in enumerate(toeplitz(own, strip_ref, 0, n_core // BLOCK)):
         here = slice(b * BLOCK, (b + 1) * BLOCK)
-        field = mm_nt(own, strip_ref[:, start : start + n_core])
         base_ref[:, here] = right_ref[:, here].astype(F32) - own[:, here].astype(F32) - field
     member_ref[...] = one_hot(labels_ref[...], member_ref.shape[0])
 
 
-def columns_kernel(*refs):
+def clear_kernel(_, columns_ref):
+    columns_ref[...] = jnp.zeros_like(columns_ref)
+
+
+def columns_kernel(_, *refs):
     parts, columns_ref = refs[:-1], refs[-1]
     n_dev = len(parts)
     targets = partners("col")
     half = parts[0].shape[0] // len(targets)
     dev = lax.axis_index("dev")
-    columns_ref[...] = jnp.zeros_like(columns_ref)
     for d, by in enumerate(targets):
         source = pl.multiple_of(by * half, half)
         for e in range(n_dev):
@@ -112,56 +123,53 @@
             columns_ref[d, pl.ds(target, half), :] = parts[e][pl.ds(source, half), :]
 
 
-def residual_kernel(unknowns, base_ref, to, ti, uo, ui, strip_ref, inv_ref, member_ref, ro, rx, ri, co, ci, res_ref):
+def residual_kernel(unknowns, base_ref, to, ti, uo, ui, strip_ref, inv_ref, member_ref, ro, rx, ri, res_ref):
     n_core = base_ref.shape[1]
     rows, shell = to.shape
     odd_row, odd_col = place("row")[1] == 1, place("col")[1] == 1
     low = [jnp.where(odd_row, ti[...], to[...]), jnp.where(odd_row, to[...], ti[...])]
     high = [jnp.where(odd_col, ui[...], uo[...]), jnp.where(odd_col, uo[...], ui[...])]
     shells = jnp.concatenate(low + high, axis=1)
-    width = shells.shape[1]
     for b in range(n_core // BLOCK):
         start = 2 * n_core - BLOCK - BLOCK * b
         here = slice(b * BLOCK, (b + 1) * BLOCK)
-        field = mm_nt(shells, strip_ref[:, start : start + width])
+        field = mm_nt(shells, strip_ref[:, start : start + shells.shape[1]])
         res_ref[:, here] = (base_ref[:, here] - field).astype(BF16)
     res = res_ref[...]
-    coarse = pack(mm_nt(res, member_ref[...]), unknowns).astype(BF16)
-    rx[...] = coarse
-    local = mm(res, inv_ref[:, n_core:]).astype(BF16)
-    back = [local[:, j * shell : (j + 1) * shell] for j in range(4)]
-    ro[:rows, :] = jnp.where(odd_row, back[1], back[0])
-    ro[rows:, :] = coarse
-    ri[:rows, :] = jnp.where(odd_row, back[0], back[1])
-    ri[rows:, :] = coarse
-    co[...] = jnp.where(odd_col, back[3], back[2])
-    ci[...] = jnp.where(odd_col, back[2], back[3])
-
-
-def partial_kernel(unknowns, columns_ref, co, ci, *refs):
+    coarse = mm_nt(res, member_ref[:unknowns, :]).astype(BF16)
+    for out in (ro, rx, ri):
+        out[-rows:, :] = jnp.zeros((rows, LANES), BF16)
+        out[-rows:, :unknowns] = coarse
+    back = mm(res, inv_ref[:, n_core : n_core + 2 * shell]).astype(BF16)
+    ro[:rows, :] = jnp.where(odd_row, back[:, shell:], back[:, :shell])
+    ri[:rows, :] = jnp.where(odd_row, back[:, :shell], back[:, shell:])
+
+
+def outer_kernel(res_ref, inv_ref, co, ci):
+    shell = co.shape[1]
+    odd_col = place("col")[1] == 1
+    back = mm(res_ref[...], inv_ref[:, -2 * shell :]).astype(BF16)
+    co[...] = jnp.where(odd_col, back[:, shell:], back[:, :shell])
+    ci[...] = jnp.where(odd_col, back[:, :shell], back[:, shell:])
+
+
+def partial_kernel(columns_ref, co, ci, *refs):
     sources = partners("row")
     n_bx = len(sources)
     gathered, outs = refs[:n_bx], refs[n_bx:]
     width = columns_ref.shape[2]
     rows = co.shape[0]
-    height = gathered[0].shape[0]
     total = jnp.zeros((rows, width), F32)
     for bx, ref in zip(sources, gathered):
-        piece = unpack(ref[-height:, :].astype(F32), unknowns)
+        piece = ref[-rows:, :].astype(F32)
         if width > LANES:
             piece = jnp.concatenate([piece, jnp.zeros((rows, width - LANES), F32)], axis=1)
-        total = total + pltpu.roll(piece, bx * unknowns, 1)
+        total = total + pltpu.roll(piece, bx * (width // n_bx), 1)
     total = total.astype(BF16)
-    outs[1][:rows, :] = co[...]
-    outs[2][:rows, :] = ci[...]
+    outs[1][:rows, :] = co[...].astype(F32)
+    outs[2][:rows, :] = ci[...].astype(F32)
     for d, out in enumerate(outs):
-        part = pack(mm_nt(total, columns_ref[d]), unknowns)
-        if d == 0:
-            out[...] = part
-        else:
-            high = part.astype(BF16)
-            out[-2 * height : -height, :] = high
-            out[-height:, :] = (part - high.astype(F32)).astype(BF16)
+        out[-rows:, :] = mm_nt(total, columns_ref[d])
 
 
 def local_kernel(res_ref, inv_ref, spots_ref, ro, ri, acc_ref):
@@ -171,36 +179,21 @@
     acc_ref[...] = mm(res_ref[...], inv_ref[:, :n_core]).astype(BF16).astype(F32) + added
 
 
-def final_kernel(unknowns, acc_ref, member_ref, spots_ref, *refs):
+def final_kernel(acc_ref, member_ref, spots_ref, *refs):
     parts, out_ref = refs[:-1], refs[-1]
     rows = acc_ref.shape[0]
-    height = parts[0].shape[0]
     solved = parts[0][...]
     for part in parts[1:]:
-        solved = solved + part[-2 * height : -height, :].astype(F32) + part[-height:, :].astype(F32)
-    solved = unpack(solved, unknowns)
+        solved = solved + part[-rows:, :]
     high = solved.astype(BF16)
     low = (solved - high.astype(F32)).astype(BF16)
     both = mm(jnp.concatenate([high, low], axis=0), member_ref[...])
-    arrived = jnp.concatenate([parts[1][:rows, :], parts[2][:rows, :]], axis=1)
+    arrived = jnp.concatenate([parts[1][:rows, :], parts[2][:rows, :]], axis=1).astype(BF16)
     added = mm_nt(arrived, spots_ref[:, arrived.shape[1] :])
     out_ref[...] = (acc_ref[...] + added + both[:rows] + both[rows:]).astype(BF16)
 
 
-def pack(value, unknowns):
-    groups = LANES // unknowns
-    height = value.shape[0] // groups
-    parts = [pltpu.roll(value[q * height : (q + 1) * height, :], q * unknowns, 1) for q in range(1, groups)]
-    return sum(parts, value[:height, :])
-
-
-def unpack(packed, unknowns):
-    keep = lax.broadcasted_iota(jnp.int32, packed.shape, 1) < unknowns
-    parts = [packed] + [pltpu.roll(packed, LANES - q * unknowns, 1) for q in range(1, LANES // unknowns)]
-    return jnp.concatenate([jnp.where(keep, part, 0.0) for part in parts], axis=0)
-
-
-def call(body, shapes, *args, hbm=(), scratch=(), limit=16, flops=10**6):
+def call(body, shapes, *args, hbm=(), scratch=(), aliases={}, limit=16, flops=10**6):
     out_shape = [jax.ShapeDtypeStruct(s, t) for s, t in shapes]
     args = [pltpu.with_memory_space_constraint(a, pltpu.HBM) if i in hbm else a for i, a in enumerate(args)]
     size = sum(a.size * a.dtype.itemsize for a in args)
@@ -210,6 +203,7 @@
         in_specs=[HBM if i in hbm else VMEM for i in range(len(args))],
         out_specs=[VMEM] * len(out_shape),
         scratch_shapes=scratch,
+        input_output_aliases=aliases,
         compiler_params=pltpu.CompilerParams(vmem_limit_bytes=limit << 20),
         cost_estimate=pl.CostEstimate(flops=flops, bytes_accessed=size, transcendentals=0),
     )(*args)
@@ -228,9 +222,7 @@
     n_bx, n_by, n_dev = (lax.axis_size(a) for a in ("row", "col", "dev"))
     coarse_rows = coarse_inverse.shape[0]
     shell = ((rows, n_shell), BF16)
-    unknowns = coarse_rows // n_bx
-    height = rows * unknowns // LANES
-    double = ((rows + height, LANES), BF16)
+    double = ((2 * rows, LANES), BF16)
 
     held = (own, right, labels, mine, kernel)
     co, ro, ci, ri, spots, own, right, labels, mine, kernel = call(
@@ -239,9 +231,10 @@
         send,
         *held,
         hbm=range(6),
-        flops=4 * 10**9,
         scratch=[pltpu.VMEM(send.shape, send.dtype), pltpu.SemaphoreType.DMA((6,))],
     )
+    column_shape = ((n_by, LANES, coarse_rows), BF16)
+    (cleared,) = call(clear_kernel, [column_shape], co, flops=8 * 10**9)
     uo = lax.ppermute(co, "col", outer_pairs(n_by))
     to = lax.ppermute(ro, "row", outer_pairs(n_bx))
     ui = lax.ppermute(ci, "col", inner_pairs(n_by))
@@ -258,9 +251,10 @@
         right,
         labels,
     )
-    ro, rx, ri, co, ci, res = call(
+    unknowns = coarse_rows // n_bx
+    ro, rx, ri, res = call(
         functools.partial(residual_kernel, unknowns),
-        [double, ((height, LANES), BF16), double, shell, shell, ((rows, n_core), BF16)],
+        [double, shell, double, ((rows, n_core), BF16)],
         base,
         to,
         ti,
@@ -273,24 +267,15 @@
     ao = lax.ppermute(ro, "row", outer_pairs(n_bx))
     rest = [lax.ppermute(rx, "row", shifted(n_bx, -o)) for o in range(2, n_bx - 1)]
     ai = lax.ppermute(ri, "row", inner_pairs(n_bx))
-    (columns,) = call(columns_kernel, [((n_by, LANES, coarse_rows), BF16)], *halves)
-    single, wide = ((2 * height, LANES), BF16), ((rows + 2 * height, LANES), BF16)
-    partials = call(
-        functools.partial(partial_kernel, unknowns),
-        [((height, LANES), F32), wide, wide] + [single] * (n_by - 3),
-        columns,
-        co,
-        ci,
-        rx,
-        ao,
-        ai,
-        *rest,
-    )
+    co, ci = call(outer_kernel, [shell, shell], res, inverse)
+    (columns,) = call(columns_kernel, [column_shape], cleared, *halves, aliases={0: 0})
+    single, wide = ((rows, LANES), F32), ((2 * rows, LANES), F32)
+    partials = call(partial_kernel, [single, wide, wide] + [single] * (n_by - 3), columns, co, ci, rx, ao, ai, *rest)
     so = lax.ppermute(partials[1], "col", outer_pairs(n_by))
     others = [lax.ppermute(partials[d + 1], "col", shifted(n_by, d)) for d in range(2, n_by - 1)]
     si = lax.ppermute(partials[2], "col", inner_pairs(n_by))
     (acc,) = call(local_kernel, [((rows, n_core), F32)], res, inverse, spots, ao, ai)
-    (out,) = call(functools.partial(final_kernel, unknowns), [((rows, n_core), BF16)], acc, member, spots, partials[0], so, si, *others)
+    (out,) = call(final_kernel, [((rows, n_core), BF16)], acc, member, spots, partials[0], so, si, *others)
     return out[:, None, None, :]
 
 

time: 24.7 us -> 26 us (1.053)
  local copies, waits for them, and re-layouts: 0.01 us -> 2.25 us
  Pallas kernels: 5.13 us -> 4.53 us
  waiting for transfers between devices: 4.41 us -> 3.96 us
    unnamed x2 -> x4, local copies, waits for them, and re-layouts: 0.01 us -> 2.24 us
    ppermute x1, starting transfers between devices: 2.5 us -> 0.68 us  [per_device(): to = lax.ppermute(ro, 'row', outer_pairs(n_bx))]
    ppermute x1, starting transfers between devices: 3.6 us -> 5.14 us  [per_device(): uo = lax.ppermute(co, 'col', outer_pairs(n_by))]
    ppermute x1, starting transfers between devices: 1.87 us -> 1.25 us  [per_device(): so = lax.ppermute(partials[1], 'col', outer_pairs(n_by))]
    pallas_call x7 -> x9, Pallas kernels: 5.13 us -> 4.53 us  [call(): pl.pallas_call(body, out_shape=out_shape, in_specs=[HBM if i in hbm else...]
    ppermute x1, starting transfers between devices: 2.58 us -> 3.17 us  [per_device(): lax.ppermute(partials[d + 1], 'col', shifted(n_by, d))]
    ppermute x1, waiting for transfers between devices: 2.03 us -> 1.51 us  [per_device(): lax.ppermute(rx, 'row', shifted(n_bx, -o))]
    ppermute x1, waiting for transfers between devices: 1.06 us -> 1.34 us  [per_device(): ui = lax.ppermute(ci, 'col', inner_pairs(n_by))]
  transfers between devices with their start and end apart: 11 -> 11, of which waited for: 3 -> 3; matrix products, arithmetic and copies ran while one was open for 0% -> 0% of each run, Pallas kernels for 10% -> 8%
where the time goes in v3:
time: 26 us; the launch traced here: 25.8 us
  starting transfers between devices  14.9 us (57%)
  Pallas kernels  4.53 us (17%)
  waiting for transfers between devices  3.96 us (15%)
  local copies, waits for them, and re-layouts  2.25 us (9%)
    ppermute x1, starting transfers between devices, per_device(): uo = lax.ppermute(co, 'col', outer_pairs(n_by))  5.14 us
    pallas_call x9, Pallas kernels, call(): pl.pallas_call(body, out_shape=out_shape, in_specs=[HBM if i in hbm else...  4.53 us
    ppermute x1, starting transfers between devices, per_device(): lax.ppermute(partials[d + 1], 'col', shifted(n_by, d))  3.17 us
    unnamed x4, local copies, waits for them, and re-layouts  2.24 us
    ppermute x1, starting transfers between devices, per_device(): lax.ppermute(rx, 'row', shifted(n_bx, -o))  1.52 us
    ppermute x1, waiting for transfers between devices, per_device(): lax.ppermute(rx, 'row', shifted(n_bx, -o))  1.51 us
    ppermute x1, starting transfers between devices, per_device(): lax.ppermute(mine, 'dev', shifted(n_dev, -e))  1.49 us
    ppermute x1, waiting for transfers between devices, per_device(): ui = lax.ppermute(ci, 'col', inner_pairs(n_by))  1.34 us
  transfers between devices with their start and end apart: 11, of which 3 were waited for; matrix products, arithmetic and copies ran while one was open for 0% of the time, Pallas kernels for 8%

profile of v3, /device:TPU:0, one launch (start us, length us, event | category | flops | bytes accessed | tf_op | source)
XLA Modules:
  0.0 25.8 jit_solution(15534768079689676271)
XLA Ops:
  0.0 1.2 %shard_map.73 = (bf16[32,128]{1,0:T(8,128)(2,1)S(1)}, bf16[32,128]{1,0:T(8,128)(2,1)S(1)}, bf16[32,128]{1,0:T(8,128)(2,1)S(1)}, bf16[32,128]{1,0:T(8,128)(2,1)S(...) custom-call(s32[4,128]{1,0:T(4,128)} %bitcast.14, ...), custom_call_target="tpu_custom_call" | custom-call | flops 1000000 | bytes 158718 | tf_op jit(solution)/shard_map/pallas_call | solution.py:200
  1.2 5.1 %collective-permute-start.2 = (bf16[32,128]{1,0:T(8,128)(2,1)S(1)}, bf16[32,128]{1,0:T(8,128)(2,1)S(1)}, u32[]{:S(2)}, u32[]{:S(2)}) collective-permute-start(bf16[32,128]{1,0:T(8,128)(2,1)S(1)} %get-tuple-element.35._), channel_id=1, source_target_pairs={{0,6},{2,4},{4,2},{6,0},{1,7},{3,5},{5,3},{7,1},{8,14},{10,12},{12... | collective-permute-start | bytes 24584 | tf_op jit(solution)/shard_map/ppermute | solution.py:238
  6.3 0.7 %collective-permute-start = (bf16[32,128]{1,0:T(8,128)(2,1)S(1)}, bf16[32,128]{1,0:T(8,128)(2,1)S(1)}, u32[]{:S(2)}, u32[]{:S(2)}) collective-permute-start(bf16[32,128]{1,0:T(8,128)(2,1)S(1)} %get-tuple-element.33), channel_id=1, source_target_pairs={{0,24},{8,16},{16,8},{24,0},{1,25},{9,17},{17,9},{25,1},{2,26},{10... | collective-permute-start | bytes 24584 | tf_op jit(solution)/shard_map/ppermute | solution.py:239
  7.0 1.0 %collective-permute-start.1 = (bf16[32,128]{1,0:T(8,128)(2,1)S(1)}, bf16[32,128]{1,0:T(8,128)(2,1)S(1)}, u32[]{:S(2)}, u32[]{:S(2)}) collective-permute-start(bf16[32,128]{1,0:T(8,128)(2,1)S(1)} %get-tuple-element.34), channel_id=1, source_target_pairs={{0,8},{8,0},{16,24},{24,16},{1,9},{9,1},{17,25},{25,17},{2,10},{10... | collective-permute-start | bytes 24584 | tf_op jit(solution)/shard_map/ppermute | solution.py:241
  8.0 0.0 collective-permute-start.3
  8.0 1.5 %collective-permute-start.6 = (bf16[64,128]{1,0:T(8,128)(2,1)S(1)}, bf16[64,128]{1,0:T(8,128)(2,1)S(1)}, u32[]{:S(2)}, u32[]{:S(2)}) collective-permute-start(bf16[64,128]{1,0:T(8,128)(2,1)S(1)} %get-tuple-element.43.refs_0_), channel_id=1, source_target_pairs={{0,1},{1,0},{2,3},{3,2},{4,5},{5,4},{6,7},{7,6},{8,9},{9,8},{10,11... | collective-permute-start | bytes 49160 | tf_op jit(solution)/shard_map/ppermute | solution.py:242
  9.5 0.1 pad_convert_fusion
  9.5 0.7 %shard_map.74 = (bf16[256,2304]{1,0:T(8,128)(2,1)S(1)}, f32[32,1024]{1,0:T(8,128)S(1)}, bf16[128,1024]{1,0:T(8,128)(2,1)S(1)}) custom-call(f32[1,2560]{1,0:T(1,128)S(1)} %reshape.kernel_ref, bf16[32,1024]{1,0:T(8,128)(2,1)S(1)} %get-tuple-element.29.own_ref, bf16[32,1024]{1,0:T(8,128)(2,1)S(1)} %get-tuple-element.30.right_ref, ...), custom_call_target="tpu_custom_call" | custom-call | flops 1000000 | bytes 145408 | tf_op jit(solution)/shard_map/pallas_call | solution.py:200
  10.2 0.0 collective-permute-done.2.uo
  10.3 0.0 collective-permute-done.to
  10.3 0.0 collective-permute-done.1.ti
  10.3 1.3 %collective-permute-done.3.ui = bf16[32,128]{1,0:T(8,128)(2,1)S(1)} collective-permute-done((bf16[32,128]{1,0:T(8,128)(2,1)S(1)}, bf16[32,128]{1,0:T(8,128)(2,1)S(1)}, u32[]{:S(2)}, u32[]{:S(2)}) %collective-permute-start.3) | collective-permute-done | bytes 8224 | tf_op jit(solution)/shard_map/ppermute | solution.py:240
  11.6 1.9 %copy-done = bf16[1,1,1024,1536]{3,2,1,0:T(8,128)(2,1)S(1)} copy-done((bf16[1,1,1024,1536]{3,2,1,0:T(8,128)(2,1)S(1)}, bf16[1,1,1024,1536]{3,2,1,0:T(8,128)(2,1)}, u32[]{:S(2)}) %copy-start) | copy-done | bytes 3145752
  13.5 0.6 %shard_map.75 = (bf16[64,128]{1,0:T(8,128)(2,1)S(1)}, bf16[32,128]{1,0:T(8,128)(2,1)S(1)}, bf16[64,128]{1,0:T(8,128)(2,1)S(1)}, bf16[32,1024]{1,0:T(8,128)(2,1)S(1)}) custom-call(f32[32,1024]{1,0:T(8,128)S(1)} %get-tuple-element.32.base_ref, bf16[32,128]{1,0:T(8,128)(2,1)S(1)} %collective-permute-done.to, bf16[32,128]{1,0:T(8,128)(2,1)S(1)} %collective-permute-done.1.ti, ...), custom_call_target="tpu_custom_call" | custom-call | flops 1000000 | bytes 4751360 | tf_op jit(solution)/shard_map/pallas_call | solution.py:200
  14.1 0.1 collective-permute-start.4
  14.2 0.6 %collective-permute-start.5 = (bf16[64,128]{1,0:T(8,128)(2,1)S(1)}, bf16[64,128]{1,0:T(8,128)(2,1)S(1)}, u32[]{:S(2)}, u32[]{:S(2)}) collective-permute-start(bf16[64,128]{1,0:T(8,128)(2,1)S(1)} %get-tuple-element.42), channel_id=1, source_target_pairs={{0,8},{8,0},{16,24},{24,16},{1,9},{9,1},{17,25},{25,17},{2,10},{10... | collective-permute-start | bytes 49160 | tf_op jit(solution)/shard_map/ppermute | solution.py:269
  14.8 1.5 %collective-permute-start.7 = (bf16[32,128]{1,0:T(8,128)(2,1)S(1)}, bf16[32,128]{1,0:T(8,128)(2,1)S(1)}, u32[]{:S(2)}, u32[]{:S(2)}) collective-permute-start(bf16[32,128]{1,0:T(8,128)(2,1)S(1)} %get-tuple-element.46.refs_0_), channel_id=1, source_target_pairs={{0,16},{8,24},{16,0},{24,8},{1,17},{9,25},{17,1},{25,9},{2,18},{10... | collective-permute-start | bytes 24584 | tf_op jit(solution)/shard_map/ppermute | solution.py:268
  16.4 0.3 %copy-done.1 = bf16[1,1,1024,1536]{3,2,1,0:T(8,128)(2,1)S(1)} copy-done((bf16[1,1,1024,1536]{3,2,1,0:T(8,128)(2,1)S(1)}, bf16[1,1,1024,1536]{3,2,1,0:T(8,128)(2,1)}, u32[]{:S(2)}) %copy-start.1) | copy-done | bytes 3145752
  16.7 0.2 shard_map.79
  16.9 0.0 collective-permute-done.6.refs_1_
  17.0 1.5 %collective-permute-done.7.refs_3_ = bf16[32,128]{1,0:T(8,128)(2,1)S(1)} collective-permute-done((bf16[32,128]{1,0:T(8,128)(2,1)S(1)}, bf16[32,128]{1,0:T(8,128)(2,1)S(1)}, u32[]{:S(2)}, u32[]{:S(2)}) %collective-permute-start.7) | collective-permute-done | bytes 8224 | tf_op jit(solution)/shard_map/ppermute | solution.py:268
  18.5 0.0 collective-permute-done.4.ro.refs_1_
  18.5 0.0 collective-permute-done.5.ri.refs_2_
  18.5 0.2 shard_map.80
  18.7 1.2 %collective-permute-start.8 = (f32[64,128]{1,0:T(8,128)S(1)}, f32[64,128]{1,0:T(8,128)S(1)}, u32[]{:S(2)}, u32[]{:S(2)}) collective-permute-start(f32[64,128]{1,0:T(8,128)S(1)} %get-tuple-element.48), channel_id=1, source_target_pairs={{0,6},{2,4},{4,2},{6,0},{1,7},{3,5},{5,3},{7,1},{8,14},{10,12},{12... | collective-permute-start | bytes 98312 | tf_op jit(solution)/shard_map/ppermute | solution.py:274
  19.9 0.0 collective-permute-start.9
  20.0 3.2 %collective-permute-start.10 = (f32[32,128]{1,0:T(8,128)S(1)}, f32[32,128]{1,0:T(8,128)S(1)}, u32[]{:S(2)}, u32[]{:S(2)}) collective-permute-start(f32[32,128]{1,0:T(8,128)S(1)} %get-tuple-element.50), channel_id=1, source_target_pairs={{0,4},{2,6},{4,0},{6,2},{1,5},{3,7},{5,1},{7,3},{8,12},{10,14},{12... | collective-permute-start | bytes 49160 | tf_op jit(solution)/shard_map/ppermute | solution.py:275
  23.1 0.6 %shard_map.76.acc_ref = f32[32,1024]{1,0:T(8,128)S(1)} custom-call(bf16[32,1024]{1,0:T(8,128)(2,1)S(1)} %get-tuple-element.39.res_ref, bf16[1024,1536]{1,0:T(8,128)(2,1)S(1)} %bitcast.9, bf16[1024,512]{1,0:T(8,128)(2,1)S(1)} %get-tuple-element.40.spots_ref, bf16[64,128]{1,0:T(8,128)(2,1)S(1)} %collective-permute-done.4.ro.refs_1_, ...), custom_call_target="tpu_custom_call" | custom-call | flops 1000000 | bytes 4292608 | tf_op jit(solution)/shard_map/pallas_call | solution.py:200
  23.7 1.1 %collective-permute-done.10.refs_3_ = f32[32,128]{1,0:T(8,128)S(1)} collective-permute-done((f32[32,128]{1,0:T(8,128)S(1)}, f32[32,128]{1,0:T(8,128)S(1)}, u32[]{:S(2)}, u32[]{:S(2)}) %collective-permute-start.10) | collective-permute-done | bytes 16416 | tf_op jit(solution)/shard_map/ppermute | solution.py:275
  24.8 0.0 collective-permute-done.8.refs_1_
  24.8 0.0 collective-permute-done.9.refs_2_
  24.8 1.0 %shard_map.81 = bf16[32,1024]{1,0:T(8,128)(2,1)} custom-call(f32[32,1024]{1,0:T(8,128)S(1)} %shard_map.76.acc_ref, bf16[128,1024]{1,0:T(8,128)(2,1)S(1)} %get-tuple-element.38.member_ref, bf16[1024,512]{1,0:T(8,128)(2,1)S(1)} %get-tuple-element.40.spots_ref, f32[32,128]{1,0:T(8,128)S(1)} %get-tuple-element.47.refs_0_, ...), custom_call_target="tpu_custom_call" | custom-call | flops 1000000 | bytes 1540096 | tf_op jit(solution)/shard_map/pallas_call | solution.py:200
  (5 shorter events, 0.1 us)
Async XLA Ops:
  1.2 9.1 %collective-permute-start.2 = (bf16[32,128]{1,0:T(8,128)(2,1)S(1)}, bf16[32,128]{1,0:T(8,128)(2,1)S(1)}, u32[]{:S(2)}, u32[]{:S(2)}) collective-permute-start(bf16[32,128]{1,0:T(8,128)(2,1)S(1)} %get-tuple-element.35._), channel_id=1, source_target_pairs={{0,6},{2,4},{4,2},{6,0},{1,7},{3,5},{5,3},{7,1},{8,14},{10,12},{12... | collective-permute-start | bytes 24584 | tf_op jit(solution)/shard_map/ppermute | solution.py:238
  6.3 3.9 %collective-permute-start = (bf16[32,128]{1,0:T(8,128)(2,1)S(1)}, bf16[32,128]{1,0:T(8,128)(2,1)S(1)}, u32[]{:S(2)}, u32[]{:S(2)}) collective-permute-start(bf16[32,128]{1,0:T(8,128)(2,1)S(1)} %get-tuple-element.33), channel_id=1, source_target_pairs={{0,24},{8,16},{16,8},{24,0},{1,25},{9,17},{17,9},{25,1},{2,26},{10... | collective-permute-start | bytes 24584 | tf_op jit(solution)/shard_map/ppermute | solution.py:239
  7.0 3.3 %collective-permute-start.1 = (bf16[32,128]{1,0:T(8,128)(2,1)S(1)}, bf16[32,128]{1,0:T(8,128)(2,1)S(1)}, u32[]{:S(2)}, u32[]{:S(2)}) collective-permute-start(bf16[32,128]{1,0:T(8,128)(2,1)S(1)} %get-tuple-element.34), channel_id=1, source_target_pairs={{0,8},{8,0},{16,24},{24,16},{1,9},{9,1},{17,25},{25,17},{2,10},{10... | collective-permute-start | bytes 24584 | tf_op jit(solution)/shard_map/ppermute | solution.py:241
  8.0 3.7 %collective-permute-start.3 = (bf16[32,128]{1,0:T(8,128)(2,1)S(1)}, bf16[32,128]{1,0:T(8,128)(2,1)S(1)}, u32[]{:S(2)}, u32[]{:S(2)}) collective-permute-start(bf16[32,128]{1,0:T(8,128)(2,1)S(1)} %get-tuple-element.36), channel_id=1, source_target_pairs={{0,2},{2,0},{4,6},{6,4},{1,3},{3,1},{5,7},{7,5},{8,10},{10,8},{12,... | collective-permute-start | bytes 24584 | tf_op jit(solution)/shard_map/ppermute | solution.py:240
  8.0 9.0 %collective-permute-start.6 = (bf16[64,128]{1,0:T(8,128)(2,1)S(1)}, bf16[64,128]{1,0:T(8,128)(2,1)S(1)}, u32[]{:S(2)}, u32[]{:S(2)}) collective-permute-start(bf16[64,128]{1,0:T(8,128)(2,1)S(1)} %get-tuple-element.43.refs_0_), channel_id=1, source_target_pairs={{0,1},{1,0},{2,3},{3,2},{4,5},{5,4},{6,7},{7,6},{8,9},{9,8},{10,11... | collective-permute-start | bytes 49160 | tf_op jit(solution)/shard_map/ppermute | solution.py:242
  11.6 1.9 %copy-start = (bf16[1,1,1024,1536]{3,2,1,0:T(8,128)(2,1)S(1)}, bf16[1,1,1024,1536]{3,2,1,0:T(8,128)(2,1)}, u32[]{:S(2)}) copy-start(bf16[1,1,1024,1536]{3,2,1,0:T(8,128)(2,1)} %param.10) | copy-start | bytes 9437188
  14.1 4.3 %collective-permute-start.4 = (bf16[64,128]{1,0:T(8,128)(2,1)S(1)}, bf16[64,128]{1,0:T(8,128)(2,1)S(1)}, u32[]{:S(2)}, u32[]{:S(2)}) collective-permute-start(bf16[64,128]{1,0:T(8,128)(2,1)S(1)} %get-tuple-element.41), channel_id=1, source_target_pairs={{0,24},{8,16},{16,8},{24,0},{1,25},{9,17},{17,9},{25,1},{2,26},{10... | collective-permute-start | bytes 49160 | tf_op jit(solution)/shard_map/ppermute | solution.py:267
  14.2 4.3 %collective-permute-start.5 = (bf16[64,128]{1,0:T(8,128)(2,1)S(1)}, bf16[64,128]{1,0:T(8,128)(2,1)S(1)}, u32[]{:S(2)}, u32[]{:S(2)}) collective-permute-start(bf16[64,128]{1,0:T(8,128)(2,1)S(1)} %get-tuple-element.42), channel_id=1, source_target_pairs={{0,8},{8,0},{16,24},{24,16},{1,9},{9,1},{17,25},{25,17},{2,10},{10... | collective-permute-start | bytes 49160 | tf_op jit(solution)/shard_map/ppermute | solution.py:269
  14.8 1.9 %copy-start.1 = (bf16[1,1,1024,1536]{3,2,1,0:T(8,128)(2,1)S(1)}, bf16[1,1,1024,1536]{3,2,1,0:T(8,128)(2,1)}, u32[]{:S(2)}) copy-start(bf16[1,1,1024,1536]{3,2,1,0:T(8,128)(2,1)} %param.10) | copy-start | bytes 9437188
  14.8 3.7 %collective-permute-start.7 = (bf16[32,128]{1,0:T(8,128)(2,1)S(1)}, bf16[32,128]{1,0:T(8,128)(2,1)S(1)}, u32[]{:S(2)}, u32[]{:S(2)}) collective-permute-start(bf16[32,128]{1,0:T(8,128)(2,1)S(1)} %get-tuple-element.46.refs_0_), channel_id=1, source_target_pairs={{0,16},{8,24},{16,0},{24,8},{1,17},{9,25},{17,1},{25,9},{2,18},{10... | collective-permute-start | bytes 24584 | tf_op jit(solution)/shard_map/ppermute | solution.py:268
  18.7 6.1 %collective-permute-start.8 = (f32[64,128]{1,0:T(8,128)S(1)}, f32[64,128]{1,0:T(8,128)S(1)}, u32[]{:S(2)}, u32[]{:S(2)}) collective-permute-start(f32[64,128]{1,0:T(8,128)S(1)} %get-tuple-element.48), channel_id=1, source_target_pairs={{0,6},{2,4},{4,2},{6,0},{1,7},{3,5},{5,3},{7,1},{8,14},{10,12},{12... | collective-permute-start | bytes 98312 | tf_op jit(solution)/shard_map/ppermute | solution.py:274
  19.9 4.9 %collective-permute-start.9 = (f32[64,128]{1,0:T(8,128)S(1)}, f32[64,128]{1,0:T(8,128)S(1)}, u32[]{:S(2)}, u32[]{:S(2)}) collective-permute-start(f32[64,128]{1,0:T(8,128)S(1)} %get-tuple-element.49), channel_id=1, source_target_pairs={{0,2},{2,0},{4,6},{6,4},{1,3},{3,1},{5,7},{7,5},{8,10},{10,8},{12,... | collective-permute-start | bytes 98312 | tf_op jit(solution)/shard_map/ppermute | solution.py:276
  20.0 4.9 %collective-permute-start.10 = (f32[32,128]{1,0:T(8,128)S(1)}, f32[32,128]{1,0:T(8,128)S(1)}, u32[]{:S(2)}, u32[]{:S(2)}) collective-permute-start(f32[32,128]{1,0:T(8,128)S(1)} %get-tuple-element.50), channel_id=1, source_target_pairs={{0,4},{2,6},{4,0},{6,2},{1,5},{3,7},{5,1},{7,3},{8,12},{10,14},{12... | collective-permute-start | bytes 49160 | tf_op jit(solution)/shard_map/ppermute | solution.py:275

commit v4 on v3

--- a/solution.py
+++ b/solution.py
@@ -90,7 +90,7 @@
         copy.wait()
 
 
-def strip_kernel(kernel_ref, own_ref, right_ref, labels_ref, strip_ref, base_ref, member_ref):
+def build_strip(kernel_ref, own_ref, right_ref, labels_ref, strip_ref, base_ref, member_ref):
     n_core = own_ref.shape[1]
     width = kernel_ref.shape[1]
     rows = 16
@@ -104,6 +104,23 @@
         here = slice(b * BLOCK, (b + 1) * BLOCK)
         base_ref[:, here] = right_ref[:, here].astype(F32) - own[:, here].astype(F32) - field
     member_ref[...] = one_hot(labels_ref[...], member_ref.shape[0])
+
+
+def is_early():
+    index, _, count = place("dev")
+    return index < count - 1
+
+
+def early_kernel(*refs):
+    @pl.when(is_early())
+    def _():
+        build_strip(*refs)
+
+
+def late_kernel(*refs):
+    @pl.when(jnp.logical_not(is_early()))
+    def _():
+        build_strip(*refs[:4], *refs[-3:])
 
 
 def clear_kernel(_, columns_ref):
@@ -153,7 +170,7 @@
     ci[...] = jnp.where(odd_col, back[:, :shell], back[:, shell:])
 
 
-def partial_kernel(columns_ref, co, ci, *refs):
+def partial_kernel(unknowns, columns_ref, co, ci, *refs):
     sources = partners("row")
     n_bx = len(sources)
     gathered, outs = refs[:n_bx], refs[n_bx:]
@@ -166,10 +183,17 @@
             piece = jnp.concatenate([piece, jnp.zeros((rows, width - LANES), F32)], axis=1)
         total = total + pltpu.roll(piece, bx * (width // n_bx), 1)
     total = total.astype(BF16)
-    outs[1][:rows, :] = co[...].astype(F32)
-    outs[2][:rows, :] = ci[...].astype(F32)
+    outs[1][:rows, :] = co[...]
+    outs[2][:rows, :] = ci[...]
+    height = outs[0].shape[0]
     for d, out in enumerate(outs):
-        out[-rows:, :] = mm_nt(total, columns_ref[d])
+        part = pack(mm_nt(total, columns_ref[d]), unknowns)
+        if d == 0:
+            out[...] = part
+        else:
+            high = part.astype(BF16)
+            out[-2 * height : -height, :] = high
+            out[-height:, :] = (part - high.astype(F32)).astype(BF16)
 
 
 def local_kernel(res_ref, inv_ref, spots_ref, ro, ri, acc_ref):
@@ -179,18 +203,33 @@
     acc_ref[...] = mm(res_ref[...], inv_ref[:, :n_core]).astype(BF16).astype(F32) + added
 
 
-def final_kernel(acc_ref, member_ref, spots_ref, *refs):
+def final_kernel(unknowns, acc_ref, member_ref, spots_ref, *refs):
     parts, out_ref = refs[:-1], refs[-1]
     rows = acc_ref.shape[0]
+    height = parts[0].shape[0]
     solved = parts[0][...]
     for part in parts[1:]:
-        solved = solved + part[-rows:, :]
+        solved = solved + part[-2 * height : -height, :].astype(F32) + part[-height:, :].astype(F32)
+    solved = unpack(solved, unknowns)
     high = solved.astype(BF16)
     low = (solved - high.astype(F32)).astype(BF16)
     both = mm(jnp.concatenate([high, low], axis=0), member_ref[...])
-    arrived = jnp.concatenate([parts[1][:rows, :], parts[2][:rows, :]], axis=1).astype(BF16)
+    arrived = jnp.concatenate([parts[1][:rows, :], parts[2][:rows, :]], axis=1)
     added = mm_nt(arrived, spots_ref[:, arrived.shape[1] :])
     out_ref[...] = (acc_ref[...] + added + both[:rows] + both[rows:]).astype(BF16)
+
+
+def pack(value, unknowns):
+    groups = LANES // unknowns
+    height = value.shape[0] // groups
+    parts = [pltpu.roll(value[q * height : (q + 1) * height, :], q * unknowns, 1) for q in range(1, groups)]
+    return sum(parts, value[:height, :])
+
+
+def unpack(packed, unknowns):
+    keep = lax.broadcasted_iota(jnp.int32, packed.shape, 1) < unknowns
+    parts = [packed] + [pltpu.roll(packed, LANES - q * unknowns, 1) for q in range(1, LANES // unknowns)]
+    return jnp.concatenate([jnp.where(keep, part, 0.0) for part in parts], axis=0)
 
 
 def call(body, shapes, *args, hbm=(), scratch=(), aliases={}, limit=16, flops=10**6):
@@ -243,14 +282,11 @@
 
     width = n_core + n_patch
     padded = jnp.pad(kernel.astype(F32), (1, width - kernel.shape[0] - 1))[None, :]
-    strip, base, member = call(
-        strip_kernel,
-        [((BLOCK, width - BLOCK), BF16), ((rows, n_core), F32), ((LANES, n_core), BF16)],
-        padded,
-        own,
-        right,
-        labels,
-    )
+    inputs = (padded, own, right, labels)
+    shapes = [((BLOCK, width - BLOCK), BF16), ((rows, n_core), F32), ((LANES, n_core), BF16)]
+    built = call(early_kernel, shapes, *inputs)
+    strip_aliases = {len(inputs) + i: i for i in range(3)}
+    strip, base, member = call(late_kernel, shapes, *inputs, *built, aliases=strip_aliases)
     unknowns = coarse_rows // n_bx
     ro, rx, ri, res = call(
         functools.partial(residual_kernel, unknowns),
@@ -269,13 +305,24 @@
     ai = lax.ppermute(ri, "row", inner_pairs(n_bx))
     co, ci = call(outer_kernel, [shell, shell], res, inverse)
     (columns,) = call(columns_kernel, [column_shape], cleared, *halves, aliases={0: 0})
-    single, wide = ((rows, LANES), F32), ((2 * rows, LANES), F32)
-    partials = call(partial_kernel, [single, wide, wide] + [single] * (n_by - 3), columns, co, ci, rx, ao, ai, *rest)
+    height = rows * unknowns // LANES
+    single, wide = ((2 * height, LANES), BF16), ((rows + 2 * height, LANES), BF16)
+    partials = call(
+        functools.partial(partial_kernel, unknowns),
+        [((height, LANES), F32), wide, wide] + [single] * (n_by - 3),
+        columns,
+        co,
+        ci,
+        rx,
+        ao,
+        ai,
+        *rest,
+    )
     so = lax.ppermute(partials[1], "col", outer_pairs(n_by))
     others = [lax.ppermute(partials[d + 1], "col", shifted(n_by, d)) for d in range(2, n_by - 1)]
     si = lax.ppermute(partials[2], "col", inner_pairs(n_by))
     (acc,) = call(local_kernel, [((rows, n_core), F32)], res, inverse, spots, ao, ai)
-    (out,) = call(final_kernel, [((rows, n_core), BF16)], acc, member, spots, partials[0], so, si, *others)
+    (out,) = call(functools.partial(final_kernel, unknowns), [((rows, n_core), BF16)], acc, member, spots, partials[0], so, si, *others)
     return out[:, None, None, :]
 
 

time: 26 us -> 26.1 us (level)
  waiting for transfers between devices: 3.96 us -> 2.29 us
  local copies, waits for them, and re-layouts: 2.25 us -> 3.77 us
    unnamed x4, local copies, waits for them, and re-layouts: 2.24 us -> 3.76 us
    ppermute x1, waiting for transfers between devices: 1.51 us -> 0.01 us  [per_device(): lax.ppermute(rx, 'row', shifted(n_bx, -o))]
    pallas_call x9 -> x10, Pallas kernels: 4.53 us -> 4.68 us  [call(): pl.pallas_call(body, out_shape=out_shape, in_specs=[HBM if i in hbm else...]
  transfers between devices with their start and end apart: 11 -> 11, of which waited for: 3 -> 2; matrix products, arithmetic and copies ran while one was open for 0% -> 0% of each run, Pallas kernels for 8% -> 9%
where the time goes in v4:
time: 26.1 us; the launch traced here: 25.9 us
  starting transfers between devices  14.9 us (57%)
  Pallas kernels  4.68 us (18%)
  local copies, waits for them, and re-layouts  3.77 us (14%)
  waiting for transfers between devices  2.29 us (9%)
    ppermute x1, starting transfers between devices, per_device(): uo = lax.ppermute(co, 'col', outer_pairs(n_by))  5.14 us
    pallas_call x10, Pallas kernels, call(): pl.pallas_call(body, out_shape=out_shape, in_specs=[HBM if i in hbm else...  4.68 us
    unnamed x4, local copies, waits for them, and re-layouts  3.76 us
    ppermute x1, starting transfers between devices, per_device(): lax.ppermute(partials[d + 1], 'col', shifted(n_by, d))  3.2 us
    ppermute x1, starting transfers between devices, per_device(): lax.ppermute(rx, 'row', shifted(n_bx, -o))  1.52 us
    ppermute x1, starting transfers between devices, per_device(): lax.ppermute(mine, 'dev', shifted(n_dev, -e))  1.49 us
    ppermute x1, waiting for transfers between devices, per_device(): ui = lax.ppermute(ci, 'col', inner_pairs(n_by))  1.31 us
    ppermute x1, starting transfers between devices, per_device(): so = lax.ppermute(partials[1], 'col', outer_pairs(n_by))  1.25 us
  transfers between devices with their start and end apart: 11, of which 2 were waited for; matrix products, arithmetic and copies ran while one was open for 0% of the time, Pallas kernels for 9%

profile of v4, /device:TPU:0, one launch (start us, length us, event | category | flops | bytes accessed | tf_op | source)
XLA Modules:
  0.0 25.9 jit_solution(17677957767103834230)
XLA Ops:
  0.0 1.2 %shard_map.73 = (bf16[32,128]{1,0:T(8,128)(2,1)S(1)}, bf16[32,128]{1,0:T(8,128)(2,1)S(1)}, bf16[32,128]{1,0:T(8,128)(2,1)S(1)}, bf16[32,128]{1,0:T(8,128)(2,1)S(...) custom-call(s32[4,128]{1,0:T(4,128)} %bitcast.14, ...), custom_call_target="tpu_custom_call" | custom-call | flops 1000000 | bytes 158718 | tf_op jit(solution)/shard_map/pallas_call | solution.py:239
  1.2 5.1 %collective-permute-start.2 = (bf16[32,128]{1,0:T(8,128)(2,1)S(1)}, bf16[32,128]{1,0:T(8,128)(2,1)S(1)}, u32[]{:S(2)}, u32[]{:S(2)}) collective-permute-start(bf16[32,128]{1,0:T(8,128)(2,1)S(1)} %get-tuple-element.41._), channel_id=1, source_target_pairs={{0,6},{2,4},{4,2},{6,0},{1,7},{3,5},{5,3},{7,1},{8,14},{10,12},{12... | collective-permute-start | bytes 24584 | tf_op jit(solution)/shard_map/ppermute | solution.py:277
  6.3 0.7 %collective-permute-start = (bf16[32,128]{1,0:T(8,128)(2,1)S(1)}, bf16[32,128]{1,0:T(8,128)(2,1)S(1)}, u32[]{:S(2)}, u32[]{:S(2)}) collective-permute-start(bf16[32,128]{1,0:T(8,128)(2,1)S(1)} %get-tuple-element.39), channel_id=1, source_target_pairs={{0,24},{8,16},{16,8},{24,0},{1,25},{9,17},{17,9},{25,1},{2,26},{10... | collective-permute-start | bytes 24584 | tf_op jit(solution)/shard_map/ppermute | solution.py:278
  7.0 1.0 %collective-permute-start.1 = (bf16[32,128]{1,0:T(8,128)(2,1)S(1)}, bf16[32,128]{1,0:T(8,128)(2,1)S(1)}, u32[]{:S(2)}, u32[]{:S(2)}) collective-permute-start(bf16[32,128]{1,0:T(8,128)(2,1)S(1)} %get-tuple-element.40), channel_id=1, source_target_pairs={{0,8},{8,0},{16,24},{24,16},{1,9},{9,1},{17,25},{25,17},{2,10},{10... | collective-permute-start | bytes 24584 | tf_op jit(solution)/shard_map/ppermute | solution.py:280
  8.0 0.0 collective-permute-start.3
  8.0 1.5 %collective-permute-start.6 = (bf16[64,128]{1,0:T(8,128)(2,1)S(1)}, bf16[64,128]{1,0:T(8,128)(2,1)S(1)}, u32[]{:S(2)}, u32[]{:S(2)}) collective-permute-start(bf16[64,128]{1,0:T(8,128)(2,1)S(1)} %get-tuple-element.49.refs_0_), channel_id=1, source_target_pairs={{0,1},{1,0},{2,3},{3,2},{4,5},{5,4},{6,7},{7,6},{8,9},{9,8},{10,11... | collective-permute-start | bytes 49160 | tf_op jit(solution)/shard_map/ppermute | solution.py:281
  9.5 0.1 pad_convert_fusion
  9.6 0.7 %shard_map.74 = (bf16[256,2304]{1,0:T(8,128)(2,1)S(1)}, f32[32,1024]{1,0:T(8,128)S(1)}, bf16[128,1024]{1,0:T(8,128)(2,1)S(1)}) custom-call(f32[1,2560]{1,0:T(1,128)S(1)} %reshape.refs_0_, bf16[32,1024]{1,0:T(8,128)(2,1)S(1)} %get-tuple-element.32.refs_1_, bf16[32,1024]{1,0:T(8,128)(2,1)S(1)} %get-tuple-element.33.refs_2_, ...), custom_call_target="tpu_custom_call" | custom-call | flops 1000000 | bytes 145408 | tf_op jit(solution)/shard_map/pallas_call | solution.py:239
  10.3 0.0 collective-permute-done.2.uo
  10.3 0.0 collective-permute-done.to
  10.3 0.0 collective-permute-done.1.ti
  10.3 1.3 %collective-permute-done.3.ui = bf16[32,128]{1,0:T(8,128)(2,1)S(1)} collective-permute-done((bf16[32,128]{1,0:T(8,128)(2,1)S(1)}, bf16[32,128]{1,0:T(8,128)(2,1)S(1)}, u32[]{:S(2)}, u32[]{:S(2)}) %collective-permute-start.3) | collective-permute-done | bytes 8224 | tf_op jit(solution)/shard_map/ppermute | solution.py:279
  11.6 1.9 %copy-done = bf16[1,1,1024,1536]{3,2,1,0:T(8,128)(2,1)S(1)} copy-done((bf16[1,1,1024,1536]{3,2,1,0:T(8,128)(2,1)S(1)}, bf16[1,1,1024,1536]{3,2,1,0:T(8,128)(2,1)}, u32[]{:S(2)}) %copy-start) | copy-done | bytes 3145752
  13.5 0.6 %shard_map.76 = (bf16[64,128]{1,0:T(8,128)(2,1)S(1)}, bf16[32,128]{1,0:T(8,128)(2,1)S(1)}, bf16[64,128]{1,0:T(8,128)(2,1)S(1)}, bf16[32,1024]{1,0:T(8,128)(2,1)S(1)}) custom-call(f32[32,1024]{1,0:T(8,128)S(1)} %get-tuple-element.38.base_ref, bf16[32,128]{1,0:T(8,128)(2,1)S(1)} %collective-permute-done.to, bf16[32,128]{1,0:T(8,128)(2,1)S(1)} %collective-permute-done.1.ti, ...), custom_call_target="tpu_custom_call" | custom-call | flops 1000000 | bytes 4751360 | tf_op jit(solution)/shard_map/pallas_call | solution.py:239
  14.1 0.1 collective-permute-start.4
  14.2 0.6 %collective-permute-start.5 = (bf16[64,128]{1,0:T(8,128)(2,1)S(1)}, bf16[64,128]{1,0:T(8,128)(2,1)S(1)}, u32[]{:S(2)}, u32[]{:S(2)}) collective-permute-start(bf16[64,128]{1,0:T(8,128)(2,1)S(1)} %get-tuple-element.48), channel_id=1, source_target_pairs={{0,8},{8,0},{16,24},{24,16},{1,9},{9,1},{17,25},{25,17},{2,10},{10... | collective-permute-start | bytes 49160 | tf_op jit(solution)/shard_map/ppermute | solution.py:305
  14.8 1.5 %collective-permute-start.7 = (bf16[32,128]{1,0:T(8,128)(2,1)S(1)}, bf16[32,128]{1,0:T(8,128)(2,1)S(1)}, u32[]{:S(2)}, u32[]{:S(2)}) collective-permute-start(bf16[32,128]{1,0:T(8,128)(2,1)S(1)} %get-tuple-element.52.refs_0_), channel_id=1, source_target_pairs={{0,16},{8,24},{16,0},{24,8},{1,17},{9,25},{17,1},{25,9},{2,18},{10... | collective-permute-start | bytes 24584 | tf_op jit(solution)/shard_map/ppermute | solution.py:304
  16.4 1.9 %copy-done.1 = bf16[1,1,1024,1536]{3,2,1,0:T(8,128)(2,1)S(1)} copy-done((bf16[1,1,1024,1536]{3,2,1,0:T(8,128)(2,1)S(1)}, bf16[1,1,1024,1536]{3,2,1,0:T(8,128)(2,1)}, u32[]{:S(2)}) %copy-start.1) | copy-done | bytes 3145752
  18.2 0.2 shard_map.80
  18.4 0.0 collective-permute-done.6.refs_1_
  18.5 0.0 collective-permute-done.7.refs_3_
  18.5 0.0 collective-permute-done.4.ro.refs_1_
  18.5 0.0 collective-permute-done.5.ri.refs_2_
  18.5 0.3 %shard_map.81 = (f32[8,128]{1,0:T(8,128)S(1)}, bf16[48,128]{1,0:T(8,128)(2,1)S(1)}, bf16[48,128]{1,0:T(8,128)(2,1)S(1)}, bf16[16,128]{1,0:T(8,128)(2,1)S(1)}) custom-call(bf16[4,128,128]{2,1,0:T(8,128)(2,1)S(1)} %shard_map.79.columns_ref, bf16[32,128]{1,0:T(8,128)(2,1)S(1)} %get-tuple-element.50.co, bf16[32,128]{1,0:T(8,128)(2,1)S(1)} %get-tuple-element.51.ci, ...), custom_call_target="tpu_custom_call" | custom-call | flops 1000000 | bytes 196608 | tf_op jit(solution)/shard_map/pallas_call | solution.py:239
  18.8 1.2 %collective-permute-start.8 = (bf16[48,128]{1,0:T(8,128)(2,1)S(1)}, bf16[48,128]{1,0:T(8,128)(2,1)S(1)}, u32[]{:S(2)}, u32[]{:S(2)}) collective-permute-start(bf16[48,128]{1,0:T(8,128)(2,1)S(1)} %get-tuple-element.54), channel_id=1, source_target_pairs={{0,6},{2,4},{4,2},{6,0},{1,7},{3,5},{5,3},{7,1},{8,14},{10,12},{12... | collective-permute-start | bytes 36872 | tf_op jit(solution)/shard_map/ppermute | solution.py:321
  20.1 0.0 collective-permute-start.9
  20.1 3.2 %collective-permute-start.10 = (bf16[16,128]{1,0:T(8,128)(2,1)S(1)}, bf16[16,128]{1,0:T(8,128)(2,1)S(1)}, u32[]{:S(2)}, u32[]{:S(2)}) collective-permute-start(bf16[16,128]{1,0:T(8,128)(2,1)S(1)} %get-tuple-element.56), channel_id=1, source_target_pairs={{0,4},{2,6},{4,0},{6,2},{1,5},{3,7},{5,1},{7,3},{8,12},{10,14},{12... | collective-permute-start | bytes 12296 | tf_op jit(solution)/shard_map/ppermute | solution.py:322
  23.3 0.6 %shard_map.77.acc_ref = f32[32,1024]{1,0:T(8,128)S(1)} custom-call(bf16[32,1024]{1,0:T(8,128)(2,1)S(1)} %get-tuple-element.45.res_ref, bf16[1024,1536]{1,0:T(8,128)(2,1)S(1)} %bitcast.9, bf16[1024,512]{1,0:T(8,128)(2,1)S(1)} %get-tuple-element.46.spots_ref, bf16[64,128]{1,0:T(8,128)(2,1)S(1)} %collective-permute-done.4.ro.refs_1_, ...), custom_call_target="tpu_custom_call" | custom-call | flops 1000000 | bytes 4292608 | tf_op jit(solution)/shard_map/pallas_call | solution.py:239
  23.9 1.0 %collective-permute-done.10.refs_3_ = bf16[16,128]{1,0:T(8,128)(2,1)S(1)} collective-permute-done((bf16[16,128]{1,0:T(8,128)(2,1)S(1)}, bf16[16,128]{1,0:T(8,128)(2,1)S(1)}, u32[]{:S(2)}, u32[]{:S(2)}) %collective-permute-start.10) | collective-permute-done | bytes 4128 | tf_op jit(solution)/shard_map/ppermute | solution.py:322
  24.9 0.0 collective-permute-done.8.refs_1_
  24.9 0.0 collective-permute-done.9.refs_2_
  24.9 1.0 %shard_map.82 = bf16[32,1024]{1,0:T(8,128)(2,1)} custom-call(f32[32,1024]{1,0:T(8,128)S(1)} %shard_map.77.acc_ref, bf16[128,1024]{1,0:T(8,128)(2,1)S(1)} %get-tuple-element.44.member_ref, bf16[1024,512]{1,0:T(8,128)(2,1)S(1)} %get-tuple-element.46.spots_ref, f32[8,128]{1,0:T(8,128)S(1)} %get-tuple-element.53.refs_0_, ...), custom_call_target="tpu_custom_call" | custom-call | flops 1000000 | bytes 1474560 | tf_op jit(solution)/shard_map/pallas_call | solution.py:239
  (6 shorter events, 0.1 us)
Async XLA Ops:
  1.2 9.1 %collective-permute-start.2 = (bf16[32,128]{1,0:T(8,128)(2,1)S(1)}, bf16[32,128]{1,0:T(8,128)(2,1)S(1)}, u32[]{:S(2)}, u32[]{:S(2)}) collective-permute-start(bf16[32,128]{1,0:T(8,128)(2,1)S(1)} %get-tuple-element.41._), channel_id=1, source_target_pairs={{0,6},{2,4},{4,2},{6,0},{1,7},{3,5},{5,3},{7,1},{8,14},{10,12},{12... | collective-permute-start | bytes 24584 | tf_op jit(solution)/shard_map/ppermute | solution.py:277
  6.3 4.0 %collective-permute-start = (bf16[32,128]{1,0:T(8,128)(2,1)S(1)}, bf16[32,128]{1,0:T(8,128)(2,1)S(1)}, u32[]{:S(2)}, u32[]{:S(2)}) collective-permute-start(bf16[32,128]{1,0:T(8,128)(2,1)S(1)} %get-tuple-element.39), channel_id=1, source_target_pairs={{0,24},{8,16},{16,8},{24,0},{1,25},{9,17},{17,9},{25,1},{2,26},{10... | collective-permute-start | bytes 24584 | tf_op jit(solution)/shard_map/ppermute | solution.py:278
  7.0 3.3 %collective-permute-start.1 = (bf16[32,128]{1,0:T(8,128)(2,1)S(1)}, bf16[32,128]{1,0:T(8,128)(2,1)S(1)}, u32[]{:S(2)}, u32[]{:S(2)}) collective-permute-start(bf16[32,128]{1,0:T(8,128)(2,1)S(1)} %get-tuple-element.40), channel_id=1, source_target_pairs={{0,8},{8,0},{16,24},{24,16},{1,9},{9,1},{17,25},{25,17},{2,10},{10... | collective-permute-start | bytes 24584 | tf_op jit(solution)/shard_map/ppermute | solution.py:280
  8.0 3.7 %collective-permute-start.3 = (bf16[32,128]{1,0:T(8,128)(2,1)S(1)}, bf16[32,128]{1,0:T(8,128)(2,1)S(1)}, u32[]{:S(2)}, u32[]{:S(2)}) collective-permute-start(bf16[32,128]{1,0:T(8,128)(2,1)S(1)} %get-tuple-element.42), channel_id=1, source_target_pairs={{0,2},{2,0},{4,6},{6,4},{1,3},{3,1},{5,7},{7,5},{8,10},{10,8},{12,... | collective-permute-start | bytes 24584 | tf_op jit(solution)/shard_map/ppermute | solution.py:279
  8.0 10.5 %collective-permute-start.6 = (bf16[64,128]{1,0:T(8,128)(2,1)S(1)}, bf16[64,128]{1,0:T(8,128)(2,1)S(1)}, u32[]{:S(2)}, u32[]{:S(2)}) collective-permute-start(bf16[64,128]{1,0:T(8,128)(2,1)S(1)} %get-tuple-element.49.refs_0_), channel_id=1, source_target_pairs={{0,1},{1,0},{2,3},{3,2},{4,5},{5,4},{6,7},{7,6},{8,9},{9,8},{10,11... | collective-permute-start | bytes 49160 | tf_op jit(solution)/shard_map/ppermute | solution.py:281
  11.6 1.9 %copy-start = (bf16[1,1,1024,1536]{3,2,1,0:T(8,128)(2,1)S(1)}, bf16[1,1,1024,1536]{3,2,1,0:T(8,128)(2,1)}, u32[]{:S(2)}) copy-start(bf16[1,1,1024,1536]{3,2,1,0:T(8,128)(2,1)} %param.10) | copy-start | bytes 9437188
  14.1 4.4 %collective-permute-start.4 = (bf16[64,128]{1,0:T(8,128)(2,1)S(1)}, bf16[64,128]{1,0:T(8,128)(2,1)S(1)}, u32[]{:S(2)}, u32[]{:S(2)}) collective-permute-start(bf16[64,128]{1,0:T(8,128)(2,1)S(1)} %get-tuple-element.47), channel_id=1, source_target_pairs={{0,24},{8,16},{16,8},{24,0},{1,25},{9,17},{17,9},{25,1},{2,26},{10... | collective-permute-start | bytes 49160 | tf_op jit(solution)/shard_map/ppermute | solution.py:303
  14.2 4.3 %collective-permute-start.5 = (bf16[64,128]{1,0:T(8,128)(2,1)S(1)}, bf16[64,128]{1,0:T(8,128)(2,1)S(1)}, u32[]{:S(2)}, u32[]{:S(2)}) collective-permute-start(bf16[64,128]{1,0:T(8,128)(2,1)S(1)} %get-tuple-element.48), channel_id=1, source_target_pairs={{0,8},{8,0},{16,24},{24,16},{1,9},{9,1},{17,25},{25,17},{2,10},{10... | collective-permute-start | bytes 49160 | tf_op jit(solution)/shard_map/ppermute | solution.py:305
  14.8 3.7 %collective-permute-start.7 = (bf16[32,128]{1,0:T(8,128)(2,1)S(1)}, bf16[32,128]{1,0:T(8,128)(2,1)S(1)}, u32[]{:S(2)}, u32[]{:S(2)}) collective-permute-start(bf16[32,128]{1,0:T(8,128)(2,1)S(1)} %get-tuple-element.52.refs_0_), channel_id=1, source_target_pairs={{0,16},{8,24},{16,0},{24,8},{1,17},{9,25},{17,1},{25,9},{2,18},{10... | collective-permute-start | bytes 24584 | tf_op jit(solution)/shard_map/ppermute | solution.py:304
  16.4 1.9 %copy-start.1 = (bf16[1,1,1024,1536]{3,2,1,0:T(8,128)(2,1)S(1)}, bf16[1,1,1024,1536]{3,2,1,0:T(8,128)(2,1)}, u32[]{:S(2)}) copy-start(bf16[1,1,1024,1536]{3,2,1,0:T(8,128)(2,1)} %param.10) | copy-start | bytes 9437188
  18.8 6.0 %collective-permute-start.8 = (bf16[48,128]{1,0:T(8,128)(2,1)S(1)}, bf16[48,128]{1,0:T(8,128)(2,1)S(1)}, u32[]{:S(2)}, u32[]{:S(2)}) collective-permute-start(bf16[48,128]{1,0:T(8,128)(2,1)S(1)} %get-tuple-element.54), channel_id=1, source_target_pairs={{0,6},{2,4},{4,2},{6,0},{1,7},{3,5},{5,3},{7,1},{8,14},{10,12},{12... | collective-permute-start | bytes 36872 | tf_op jit(solution)/shard_map/ppermute | solution.py:321
  20.1 4.8 %collective-permute-start.9 = (bf16[48,128]{1,0:T(8,128)(2,1)S(1)}, bf16[48,128]{1,0:T(8,128)(2,1)S(1)}, u32[]{:S(2)}, u32[]{:S(2)}) collective-permute-start(bf16[48,128]{1,0:T(8,128)(2,1)S(1)} %get-tuple-element.55), channel_id=1, source_target_pairs={{0,2},{2,0},{4,6},{6,4},{1,3},{3,1},{5,7},{7,5},{8,10},{10,8},{12,... | collective-permute-start | bytes 36872 | tf_op jit(solution)/shard_map/ppermute | solution.py:323
  20.1 4.8 %collective-permute-start.10 = (bf16[16,128]{1,0:T(8,128)(2,1)S(1)}, bf16[16,128]{1,0:T(8,128)(2,1)S(1)}, u32[]{:S(2)}, u32[]{:S(2)}) collective-permute-start(bf16[16,128]{1,0:T(8,128)(2,1)S(1)} %get-tuple-element.56), channel_id=1, source_target_pairs={{0,4},{2,6},{4,0},{6,2},{1,5},{3,7},{5,1},{7,3},{8,12},{10,14},{12... | collective-permute-start | bytes 12296 | tf_op jit(solution)/shard_map/ppermute | solution.py:322

commit v5 on v4

--- a/solution.py
+++ b/solution.py
@@ -75,17 +75,16 @@
     copies[0].wait()
     n_core = own_ref.shape[1]
     shell = send_ref.shape[1]
-    hots = []
-    for slot, (axis, base, inner) in enumerate((("row", 0, 0), ("row", 0, 1), ("col", 2, 0), ("col", 2, 1))):
+    labels = []
+    for axis, base in (("row", 0), ("col", 2)):
         odd = place(axis)[1]
-        direction = base + jnp.where(odd == 1, inner, 1 - inner)
-        hot = one_hot(send_ref[pl.ds(direction, 1), :], n_core)
-        spots_ref[:, slot * shell : (slot + 1) * shell] = hot
-        hots.append(hot)
+        labels += [send_ref[pl.ds(base + 1 - odd, 1), :], send_ref[pl.ds(base + odd, 1), :]]
+    for slot, label in enumerate(labels):
+        spots_ref[:, slot * shell : (slot + 1) * shell] = one_hot(label, n_core)
     copies[1].wait()
-    own = own_ref[...]
-    for slot, out in ((2, co), (0, ro), (3, ci), (1, ri)):
-        out[...] = mm(own, spots_ref[:, slot * shell : (slot + 1) * shell]).astype(BF16)
+    sent = mm(own_ref[...], spots_ref[...]).astype(BF16)
+    for slot, out in enumerate((ro, ri, co, ci)):
+        out[...] = sent[:, slot * shell : (slot + 1) * shell]
     for copy in copies[2:]:
         copy.wait()
 

time: 26.1 us -> 26.1 us (level)
  no operation moved by 1% of the time
where the time goes in v5:
time: 26.1 us; the launch traced here: 25.9 us
  starting transfers between devices  14.9 us (57%)
  Pallas kernels  4.71 us (18%)
  local copies, waits for them, and re-layouts  3.77 us (14%)
  waiting for transfers between devices  2.29 us (9%)
    ppermute x1, starting transfers between devices, per_device(): uo = lax.ppermute(co, 'col', outer_pairs(n_by))  5.14 us
    pallas_call x10, Pallas kernels, call(): pl.pallas_call(body, out_shape=out_shape, in_specs=[HBM if i in hbm else...  4.71 us
    unnamed x4, local copies, waits for them, and re-layouts  3.76 us
    ppermute x1, starting transfers between devices, per_device(): lax.ppermute(partials[d + 1], 'col', shifted(n_by, d))  3.2 us
    ppermute x1, starting transfers between devices, per_device(): lax.ppermute(rx, 'row', shifted(n_bx, -o))  1.52 us
    ppermute x1, starting transfers between devices, per_device(): lax.ppermute(mine, 'dev', shifted(n_dev, -e))  1.49 us
    ppermute x1, waiting for transfers between devices, per_device(): ui = lax.ppermute(ci, 'col', inner_pairs(n_by))  1.31 us
    ppermute x1, starting transfers between devices, per_device(): so = lax.ppermute(partials[1], 'col', outer_pairs(n_by))  1.25 us
  transfers between devices with their start and end apart: 11, of which 2 were waited for; matrix products, arithmetic and copies ran while one was open for 0% of the time, Pallas kernels for 9%

profile of v5, /device:TPU:0, one launch (start us, length us, event | category | flops | bytes accessed | tf_op | source)
XLA Modules:
  0.0 25.9 jit_solution(10960452544436068460)
XLA Ops:
  0.0 1.2 %shard_map.73 = (bf16[32,128]{1,0:T(8,128)(2,1)S(1)}, bf16[32,128]{1,0:T(8,128)(2,1)S(1)}, bf16[32,128]{1,0:T(8,128)(2,1)S(1)}, bf16[32,128]{1,0:T(8,128)(2,1)S(...) custom-call(s32[4,128]{1,0:T(4,128)} %bitcast.14, ...), custom_call_target="tpu_custom_call" | custom-call | flops 1000000 | bytes 158718 | tf_op jit(solution)/shard_map/pallas_call | solution.py:238
  1.2 5.1 %collective-permute-start.2 = (bf16[32,128]{1,0:T(8,128)(2,1)S(1)}, bf16[32,128]{1,0:T(8,128)(2,1)S(1)}, u32[]{:S(2)}, u32[]{:S(2)}) collective-permute-start(bf16[32,128]{1,0:T(8,128)(2,1)S(1)} %get-tuple-element.41._), channel_id=1, source_target_pairs={{0,6},{2,4},{4,2},{6,0},{1,7},{3,5},{5,3},{7,1},{8,14},{10,12},{12... | collective-permute-start | bytes 24584 | tf_op jit(solution)/shard_map/ppermute | solution.py:276
  6.4 0.7 %collective-permute-start = (bf16[32,128]{1,0:T(8,128)(2,1)S(1)}, bf16[32,128]{1,0:T(8,128)(2,1)S(1)}, u32[]{:S(2)}, u32[]{:S(2)}) collective-permute-start(bf16[32,128]{1,0:T(8,128)(2,1)S(1)} %get-tuple-element.39), channel_id=1, source_target_pairs={{0,24},{8,16},{16,8},{24,0},{1,25},{9,17},{17,9},{25,1},{2,26},{10... | collective-permute-start | bytes 24584 | tf_op jit(solution)/shard_map/ppermute | solution.py:277
  7.0 1.0 %collective-permute-start.1 = (bf16[32,128]{1,0:T(8,128)(2,1)S(1)}, bf16[32,128]{1,0:T(8,128)(2,1)S(1)}, u32[]{:S(2)}, u32[]{:S(2)}) collective-permute-start(bf16[32,128]{1,0:T(8,128)(2,1)S(1)} %get-tuple-element.40), channel_id=1, source_target_pairs={{0,8},{8,0},{16,24},{24,16},{1,9},{9,1},{17,25},{25,17},{2,10},{10... | collective-permute-start | bytes 24584 | tf_op jit(solution)/shard_map/ppermute | solution.py:279
  8.0 0.0 collective-permute-start.3
  8.0 1.5 %collective-permute-start.6 = (bf16[64,128]{1,0:T(8,128)(2,1)S(1)}, bf16[64,128]{1,0:T(8,128)(2,1)S(1)}, u32[]{:S(2)}, u32[]{:S(2)}) collective-permute-start(bf16[64,128]{1,0:T(8,128)(2,1)S(1)} %get-tuple-element.49.refs_0_), channel_id=1, source_target_pairs={{0,1},{1,0},{2,3},{3,2},{4,5},{5,4},{6,7},{7,6},{8,9},{9,8},{10,11... | collective-permute-start | bytes 49160 | tf_op jit(solution)/shard_map/ppermute | solution.py:280
  9.5 0.1 pad_convert_fusion
  9.6 0.7 %shard_map.74 = (bf16[256,2304]{1,0:T(8,128)(2,1)S(1)}, f32[32,1024]{1,0:T(8,128)S(1)}, bf16[128,1024]{1,0:T(8,128)(2,1)S(1)}) custom-call(f32[1,2560]{1,0:T(1,128)S(1)} %reshape.refs_0_, bf16[32,1024]{1,0:T(8,128)(2,1)S(1)} %get-tuple-element.32.refs_1_, bf16[32,1024]{1,0:T(8,128)(2,1)S(1)} %get-tuple-element.33.refs_2_, ...), custom_call_target="tpu_custom_call" | custom-call | flops 1000000 | bytes 145408 | tf_op jit(solution)/shard_map/pallas_call | solution.py:238
  10.3 0.0 collective-permute-done.2.uo
  10.3 0.0 collective-permute-done.to
  10.3 0.0 collective-permute-done.1.ti
  10.3 1.3 %collective-permute-done.3.ui = bf16[32,128]{1,0:T(8,128)(2,1)S(1)} collective-permute-done((bf16[32,128]{1,0:T(8,128)(2,1)S(1)}, bf16[32,128]{1,0:T(8,128)(2,1)S(1)}, u32[]{:S(2)}, u32[]{:S(2)}) %collective-permute-start.3) | collective-permute-done | bytes 8224 | tf_op jit(solution)/shard_map/ppermute | solution.py:278
  11.6 1.9 %copy-done = bf16[1,1,1024,1536]{3,2,1,0:T(8,128)(2,1)S(1)} copy-done((bf16[1,1,1024,1536]{3,2,1,0:T(8,128)(2,1)S(1)}, bf16[1,1,1024,1536]{3,2,1,0:T(8,128)(2,1)}, u32[]{:S(2)}) %copy-start) | copy-done | bytes 3145752
  13.5 0.6 %shard_map.76 = (bf16[64,128]{1,0:T(8,128)(2,1)S(1)}, bf16[32,128]{1,0:T(8,128)(2,1)S(1)}, bf16[64,128]{1,0:T(8,128)(2,1)S(1)}, bf16[32,1024]{1,0:T(8,128)(2,1)S(1)}) custom-call(f32[32,1024]{1,0:T(8,128)S(1)} %get-tuple-element.38.base_ref, bf16[32,128]{1,0:T(8,128)(2,1)S(1)} %collective-permute-done.to, bf16[32,128]{1,0:T(8,128)(2,1)S(1)} %collective-permute-done.1.ti, ...), custom_call_target="tpu_custom_call" | custom-call | flops 1000000 | bytes 4751360 | tf_op jit(solution)/shard_map/pallas_call | solution.py:238
  14.2 0.1 collective-permute-start.4
  14.2 0.6 %collective-permute-start.5 = (bf16[64,128]{1,0:T(8,128)(2,1)S(1)}, bf16[64,128]{1,0:T(8,128)(2,1)S(1)}, u32[]{:S(2)}, u32[]{:S(2)}) collective-permute-start(bf16[64,128]{1,0:T(8,128)(2,1)S(1)} %get-tuple-element.48), channel_id=1, source_target_pairs={{0,8},{8,0},{16,24},{24,16},{1,9},{9,1},{17,25},{25,17},{2,10},{10... | collective-permute-start | bytes 49160 | tf_op jit(solution)/shard_map/ppermute | solution.py:304
  14.9 1.5 %collective-permute-start.7 = (bf16[32,128]{1,0:T(8,128)(2,1)S(1)}, bf16[32,128]{1,0:T(8,128)(2,1)S(1)}, u32[]{:S(2)}, u32[]{:S(2)}) collective-permute-start(bf16[32,128]{1,0:T(8,128)(2,1)S(1)} %get-tuple-element.52.refs_0_), channel_id=1, source_target_pairs={{0,16},{8,24},{16,0},{24,8},{1,17},{9,25},{17,1},{25,9},{2,18},{10... | collective-permute-start | bytes 24584 | tf_op jit(solution)/shard_map/ppermute | solution.py:303
  16.4 1.9 %copy-done.1 = bf16[1,1,1024,1536]{3,2,1,0:T(8,128)(2,1)S(1)} copy-done((bf16[1,1,1024,1536]{3,2,1,0:T(8,128)(2,1)S(1)}, bf16[1,1,1024,1536]{3,2,1,0:T(8,128)(2,1)}, u32[]{:S(2)}) %copy-start.1) | copy-done | bytes 3145752
  18.3 0.2 shard_map.80
  18.5 0.0 collective-permute-done.6.refs_1_
  18.5 0.0 collective-permute-done.7.refs_3_
  18.5 0.0 collective-permute-done.4.ro.refs_1_
  18.5 0.0 collective-permute-done.5.ri.refs_2_
  18.5 0.3 %shard_map.81 = (f32[8,128]{1,0:T(8,128)S(1)}, bf16[48,128]{1,0:T(8,128)(2,1)S(1)}, bf16[48,128]{1,0:T(8,128)(2,1)S(1)}, bf16[16,128]{1,0:T(8,128)(2,1)S(1)}) custom-call(bf16[4,128,128]{2,1,0:T(8,128)(2,1)S(1)} %shard_map.79.columns_ref, bf16[32,128]{1,0:T(8,128)(2,1)S(1)} %get-tuple-element.50.co, bf16[32,128]{1,0:T(8,128)(2,1)S(1)} %get-tuple-element.51.ci, ...), custom_call_target="tpu_custom_call" | custom-call | flops 1000000 | bytes 196608 | tf_op jit(solution)/shard_map/pallas_call | solution.py:238
  18.8 1.2 %collective-permute-start.8 = (bf16[48,128]{1,0:T(8,128)(2,1)S(1)}, bf16[48,128]{1,0:T(8,128)(2,1)S(1)}, u32[]{:S(2)}, u32[]{:S(2)}) collective-permute-start(bf16[48,128]{1,0:T(8,128)(2,1)S(1)} %get-tuple-element.54), channel_id=1, source_target_pairs={{0,6},{2,4},{4,2},{6,0},{1,7},{3,5},{5,3},{7,1},{8,14},{10,12},{12... | collective-permute-start | bytes 36872 | tf_op jit(solution)/shard_map/ppermute | solution.py:320
  20.1 0.0 collective-permute-start.9
  20.1 3.2 %collective-permute-start.10 = (bf16[16,128]{1,0:T(8,128)(2,1)S(1)}, bf16[16,128]{1,0:T(8,128)(2,1)S(1)}, u32[]{:S(2)}, u32[]{:S(2)}) collective-permute-start(bf16[16,128]{1,0:T(8,128)(2,1)S(1)} %get-tuple-element.56), channel_id=1, source_target_pairs={{0,4},{2,6},{4,0},{6,2},{1,5},{3,7},{5,1},{7,3},{8,12},{10,14},{12... | collective-permute-start | bytes 12296 | tf_op jit(solution)/shard_map/ppermute | solution.py:321
  23.3 0.6 %shard_map.77.acc_ref = f32[32,1024]{1,0:T(8,128)S(1)} custom-call(bf16[32,1024]{1,0:T(8,128)(2,1)S(1)} %get-tuple-element.45.res_ref, bf16[1024,1536]{1,0:T(8,128)(2,1)S(1)} %bitcast.9, bf16[1024,512]{1,0:T(8,128)(2,1)S(1)} %get-tuple-element.46.spots_ref, bf16[64,128]{1,0:T(8,128)(2,1)S(1)} %collective-permute-done.4.ro.refs_1_, ...), custom_call_target="tpu_custom_call" | custom-call | flops 1000000 | bytes 4292608 | tf_op jit(solution)/shard_map/pallas_call | solution.py:238
  23.9 1.0 %collective-permute-done.10.refs_3_ = bf16[16,128]{1,0:T(8,128)(2,1)S(1)} collective-permute-done((bf16[16,128]{1,0:T(8,128)(2,1)S(1)}, bf16[16,128]{1,0:T(8,128)(2,1)S(1)}, u32[]{:S(2)}, u32[]{:S(2)}) %collective-permute-start.10) | collective-permute-done | bytes 4128 | tf_op jit(solution)/shard_map/ppermute | solution.py:321
  24.9 0.0 collective-permute-done.8.refs_1_
  24.9 0.0 collective-permute-done.9.refs_2_
  24.9 1.0 %shard_map.82 = bf16[32,1024]{1,0:T(8,128)(2,1)} custom-call(f32[32,1024]{1,0:T(8,128)S(1)} %shard_map.77.acc_ref, bf16[128,1024]{1,0:T(8,128)(2,1)S(1)} %get-tuple-element.44.member_ref, bf16[1024,512]{1,0:T(8,128)(2,1)S(1)} %get-tuple-element.46.spots_ref, f32[8,128]{1,0:T(8,128)S(1)} %get-tuple-element.53.refs_0_, ...), custom_call_target="tpu_custom_call" | custom-call | flops 1000000 | bytes 1474560 | tf_op jit(solution)/shard_map/pallas_call | solution.py:238
  (6 shorter events, 0.1 us)
Async XLA Ops:
  1.2 9.1 %collective-permute-start.2 = (bf16[32,128]{1,0:T(8,128)(2,1)S(1)}, bf16[32,128]{1,0:T(8,128)(2,1)S(1)}, u32[]{:S(2)}, u32[]{:S(2)}) collective-permute-start(bf16[32,128]{1,0:T(8,128)(2,1)S(1)} %get-tuple-element.41._), channel_id=1, source_target_pairs={{0,6},{2,4},{4,2},{6,0},{1,7},{3,5},{5,3},{7,1},{8,14},{10,12},{12... | collective-permute-start | bytes 24584 | tf_op jit(solution)/shard_map/ppermute | solution.py:276
  6.4 4.0 %collective-permute-start = (bf16[32,128]{1,0:T(8,128)(2,1)S(1)}, bf16[32,128]{1,0:T(8,128)(2,1)S(1)}, u32[]{:S(2)}, u32[]{:S(2)}) collective-permute-start(bf16[32,128]{1,0:T(8,128)(2,1)S(1)} %get-tuple-element.39), channel_id=1, source_target_pairs={{0,24},{8,16},{16,8},{24,0},{1,25},{9,17},{17,9},{25,1},{2,26},{10... | collective-permute-start | bytes 24584 | tf_op jit(solution)/shard_map/ppermute | solution.py:277
  7.0 3.3 %collective-permute-start.1 = (bf16[32,128]{1,0:T(8,128)(2,1)S(1)}, bf16[32,128]{1,0:T(8,128)(2,1)S(1)}, u32[]{:S(2)}, u32[]{:S(2)}) collective-permute-start(bf16[32,128]{1,0:T(8,128)(2,1)S(1)} %get-tuple-element.40), channel_id=1, source_target_pairs={{0,8},{8,0},{16,24},{24,16},{1,9},{9,1},{17,25},{25,17},{2,10},{10... | collective-permute-start | bytes 24584 | tf_op jit(solution)/shard_map/ppermute | solution.py:279
  8.0 3.7 %collective-permute-start.3 = (bf16[32,128]{1,0:T(8,128)(2,1)S(1)}, bf16[32,128]{1,0:T(8,128)(2,1)S(1)}, u32[]{:S(2)}, u32[]{:S(2)}) collective-permute-start(bf16[32,128]{1,0:T(8,128)(2,1)S(1)} %get-tuple-element.42), channel_id=1, source_target_pairs={{0,2},{2,0},{4,6},{6,4},{1,3},{3,1},{5,7},{7,5},{8,10},{10,8},{12,... | collective-permute-start | bytes 24584 | tf_op jit(solution)/shard_map/ppermute | solution.py:278
  8.0 10.5 %collective-permute-start.6 = (bf16[64,128]{1,0:T(8,128)(2,1)S(1)}, bf16[64,128]{1,0:T(8,128)(2,1)S(1)}, u32[]{:S(2)}, u32[]{:S(2)}) collective-permute-start(bf16[64,128]{1,0:T(8,128)(2,1)S(1)} %get-tuple-element.49.refs_0_), channel_id=1, source_target_pairs={{0,1},{1,0},{2,3},{3,2},{4,5},{5,4},{6,7},{7,6},{8,9},{9,8},{10,11... | collective-permute-start | bytes 49160 | tf_op jit(solution)/shard_map/ppermute | solution.py:280
  11.6 1.9 %copy-start = (bf16[1,1,1024,1536]{3,2,1,0:T(8,128)(2,1)S(1)}, bf16[1,1,1024,1536]{3,2,1,0:T(8,128)(2,1)}, u32[]{:S(2)}) copy-start(bf16[1,1,1024,1536]{3,2,1,0:T(8,128)(2,1)} %param.10) | copy-start | bytes 9437188
  14.2 4.4 %collective-permute-start.4 = (bf16[64,128]{1,0:T(8,128)(2,1)S(1)}, bf16[64,128]{1,0:T(8,128)(2,1)S(1)}, u32[]{:S(2)}, u32[]{:S(2)}) collective-permute-start(bf16[64,128]{1,0:T(8,128)(2,1)S(1)} %get-tuple-element.47), channel_id=1, source_target_pairs={{0,24},{8,16},{16,8},{24,0},{1,25},{9,17},{17,9},{25,1},{2,26},{10... | collective-permute-start | bytes 49160 | tf_op jit(solution)/shard_map/ppermute | solution.py:302
  14.2 4.3 %collective-permute-start.5 = (bf16[64,128]{1,0:T(8,128)(2,1)S(1)}, bf16[64,128]{1,0:T(8,128)(2,1)S(1)}, u32[]{:S(2)}, u32[]{:S(2)}) collective-permute-start(bf16[64,128]{1,0:T(8,128)(2,1)S(1)} %get-tuple-element.48), channel_id=1, source_target_pairs={{0,8},{8,0},{16,24},{24,16},{1,9},{9,1},{17,25},{25,17},{2,10},{10... | collective-permute-start | bytes 49160 | tf_op jit(solution)/shard_map/ppermute | solution.py:304
  14.9 3.7 %collective-permute-start.7 = (bf16[32,128]{1,0:T(8,128)(2,1)S(1)}, bf16[32,128]{1,0:T(8,128)(2,1)S(1)}, u32[]{:S(2)}, u32[]{:S(2)}) collective-permute-start(bf16[32,128]{1,0:T(8,128)(2,1)S(1)} %get-tuple-element.52.refs_0_), channel_id=1, source_target_pairs={{0,16},{8,24},{16,0},{24,8},{1,17},{9,25},{17,1},{25,9},{2,18},{10... | collective-permute-start | bytes 24584 | tf_op jit(solution)/shard_map/ppermute | solution.py:303
  16.4 1.9 %copy-start.1 = (bf16[1,1,1024,1536]{3,2,1,0:T(8,128)(2,1)S(1)}, bf16[1,1,1024,1536]{3,2,1,0:T(8,128)(2,1)}, u32[]{:S(2)}) copy-start(bf16[1,1,1024,1536]{3,2,1,0:T(8,128)(2,1)} %param.10) | copy-start | bytes 9437188
  18.8 6.0 %collective-permute-start.8 = (bf16[48,128]{1,0:T(8,128)(2,1)S(1)}, bf16[48,128]{1,0:T(8,128)(2,1)S(1)}, u32[]{:S(2)}, u32[]{:S(2)}) collective-permute-start(bf16[48,128]{1,0:T(8,128)(2,1)S(1)} %get-tuple-element.54), channel_id=1, source_target_pairs={{0,6},{2,4},{4,2},{6,0},{1,7},{3,5},{5,3},{7,1},{8,14},{10,12},{12... | collective-permute-start | bytes 36872 | tf_op jit(solution)/shard_map/ppermute | solution.py:320
  20.1 4.8 %collective-permute-start.9 = (bf16[48,128]{1,0:T(8,128)(2,1)S(1)}, bf16[48,128]{1,0:T(8,128)(2,1)S(1)}, u32[]{:S(2)}, u32[]{:S(2)}) collective-permute-start(bf16[48,128]{1,0:T(8,128)(2,1)S(1)} %get-tuple-element.55), channel_id=1, source_target_pairs={{0,2},{2,0},{4,6},{6,4},{1,3},{3,1},{5,7},{7,5},{8,10},{10,8},{12,... | collective-permute-start | bytes 36872 | tf_op jit(solution)/shard_map/ppermute | solution.py:322
  20.1 4.8 %collective-permute-start.10 = (bf16[16,128]{1,0:T(8,128)(2,1)S(1)}, bf16[16,128]{1,0:T(8,128)(2,1)S(1)}, u32[]{:S(2)}, u32[]{:S(2)}) collective-permute-start(bf16[16,128]{1,0:T(8,128)(2,1)S(1)} %get-tuple-element.56), channel_id=1, source_target_pairs={{0,4},{2,6},{4,0},{6,2},{1,5},{3,7},{5,1},{7,3},{8,12},{10,14},{12... | collective-permute-start | bytes 12296 | tf_op jit(solution)/shard_map/ppermute | solution.py:321
